TPU v7x, 32 devices: a whole 2x2x4 slice. The times are simulated.
32 devices in a mesh: dp: 8 (over z, x), feat: 4 (over y, core).
Axes of the slice: x: 2, y: 2, z: 4, core: 2. Of those that a mesh axis runs over, the one named last changes fastest.
Arguments:
- tokens: bfloat16 [4096, 1024], P('dp', 'feat'), may hold values from -6 to 6
- doc_lengths: int32 [16, 3], P('dp'), may hold values from 1 to 128, 256 in all within a row
- norm_gain: bfloat16 [1024], P('feat'), may hold values from 0.5 to 1.5
- norm_shift: bfloat16 [1024], P('feat'), may hold values from -1.25 to 1.25
- qkv_weight: bfloat16 [1024, 3, 1024], P('dp', None, 'feat'), may hold values from -0.1875 to 0.1875
- qkv_bias: bfloat16 [3, 1024], P(None, 'feat'), may hold values from -1.75 to 1.75
- omega: float32 [64, 64], replicated, may hold values from -4 to 4
- qmc_weights: float32 [64], replicated, may hold values from 0.5 to 2
- out_weight: bfloat16 [1024, 1024], P('feat', 'dp'), may hold values from -1.5 to 1.5
- out_bias: bfloat16 [1024], P('feat'), may hold values from -1.75 to 1.75
- up_weight: bfloat16 [1024, 4096], P('dp', 'feat'), may hold values from -0.1875 to 0.1875
- up_bias: bfloat16 [4096], P('feat'), may hold values from -1.75 to 1.75
- down_weight: bfloat16 [4096, 1024], P('feat', 'dp'), may hold values from -0.09375 to 0.09375
- out_grad: bfloat16 [4096, 1024], P('dp', 'feat'), may hold values from -6 to 6
Outputs:
- block_out: bfloat16 [4096, 1024], P('dp', 'feat')
- input_grad: bfloat16 [4096, 1024], P('dp', 'feat')
- gain_grad: float32 [1024], P('feat')
- shift_grad: float32 [1024], P('feat')
- qkv_weight_grad: float32 [1024, 3, 1024], P('dp', None, 'feat')
- qkv_bias_grad: float32 [3, 1024], P(None, 'feat')
- out_weight_grad: float32 [1024, 1024], P('feat', 'dp')
- out_bias_grad: float32 [1024], P('feat')
- up_weight_grad: float32 [1024, 4096], P('dp', 'feat')
- up_bias_grad: float32 [4096], P('feat')
- down_weight_grad: float32 [4096, 1024], P('feat', 'dp')
Inputs may be any that keep to these rules, and one draw needn't show every extreme that they name: `doc_lengths`: each row lists the lengths of the 3 sequences of one micro-batch; they sum to 256, and the longest is exactly 128.
All inputs are finite; a program needn't handle non-finite values.
Results may differ from a plain program's by a relative error of at most 0.013.
The roundings to bfloat16 on the way count: a program that leaves them out, or rounds other values in their place, can miss the bound.
Values may be sent and summed in bfloat16 or wider, within the bound.
A program may use at most 128 MiB of HBM per device.

v0:
```python
import math

import jax
import jax.numpy as jnp
from jax import lax
from jax.sharding import PartitionSpec as P

D = 1024
HD = 64
ROT = 16
M = 64
SPAN = 64
MB = 2


epsilon = 1e-05
highest = lax.Precision.HIGHEST


def row_layout(lengths, row_count):
    seq_ends = jnp.cumsum(lengths)
    starts = seq_ends - lengths
    row_ids = jnp.arange(row_count, dtype=jnp.int32)
    segment = jnp.sum((row_ids[:, None] >= seq_ends[None, :]).astype(jnp.int32), 1)
    belongs = segment[:, None] == jnp.arange(lengths.shape[0], dtype=jnp.int32)[None, :]
    row_begin = jnp.sum(jnp.where(belongs, starts[None, :], 0), 1)
    return (segment, (row_ids - row_begin).astype(jnp.float32))


def rotate(vectors, positions):
    half_rot = ROT // 2
    inv_freq = jnp.exp(-jnp.arange(half_rot, dtype=jnp.float32) * (2.0 / ROT) * math.log(10000.0))
    angles = positions[:, None] * inv_freq[None, :]
    cosine = jnp.cos(angles)[:, None, :]
    sine = jnp.sin(angles)[:, None, :]
    lower_part = vectors[..., :half_rot]
    upper_part = vectors[..., half_rot:ROT]
    return jnp.concatenate(
        [
            lower_part * cosine - upper_part * sine,
            upper_part * cosine + lower_part * sine,
            vectors[..., ROT:],
        ],
        -1,
    )


def dct_table():
    ramp_vals = jnp.arange(HD, dtype=jnp.float32)
    weights_row = jnp.where(ramp_vals == 0.0, jnp.sqrt(1.0 / HD), jnp.sqrt(2.0 / HD))
    return (
        jnp.cos(math.pi * (2.0 * ramp_vals[None, :] + 1.0) * ramp_vals[:, None] / (2.0 * HD))
        * weights_row[:, None]
    )


def feature_map(vectors, positions, omega):
    turned = rotate(vectors, positions) * HD ** (-0.25)
    spectrum = jnp.einsum("rhn,kn->rhk", turned, dct_table(), precision=highest)
    scores = jnp.einsum("rhk,kj->rhj", spectrum, omega, precision=highest)
    return jnp.exp(scores - 0.5 * jnp.sum(turned * turned, -1, keepdims=True))


def both_maps(queries, keys_raw, positions, omega_used, weights_used):
    return (
        weights_used * feature_map(queries, positions, omega_used),
        feature_map(keys_raw, positions, omega_used),
    )


def gelu_exact(pre_act):
    return jax.nn.gelu(pre_act, approximate=False)


def block_masks(segment):
    nblocks = segment.shape[0] // SPAN
    blocks = segment.reshape(nblocks, SPAN)
    head_seg = blocks[:, 0]
    following = jnp.concatenate([head_seg[1:], jnp.full((1,), -1, jnp.int32)])
    carry_keep = (head_seg == following).astype(jnp.float32)
    row_gate = (blocks == head_seg[:, None]).astype(jnp.float32)
    chosen = (blocks == following[:, None]).astype(jnp.float32)
    offsets_in = jnp.arange(SPAN, dtype=jnp.int32)
    causal = offsets_in[:, None] >= offsets_in[None, :]
    same_seq = blocks[:, :, None] == blocks[:, None, :]
    block_mask = (causal[None] & same_seq).astype(jnp.float32)
    return (carry_keep, row_gate, chosen, block_mask)


def carry_chain(carry_keep, increments):

    def combine(earlier, latter):
        return (earlier[0] * latter[0], latter[0] * earlier[1] + latter[1])

    factors = jnp.broadcast_to(carry_keep[:, None, None, None], increments.shape)
    return lax.associative_scan(combine, (factors, increments))[1]


def block_states(carry_keep, picked, block_v):
    increments = jnp.einsum("bshj,bshe->bhje", picked, block_v, precision=highest)
    totals = carry_chain(carry_keep, increments)
    return jnp.concatenate([jnp.zeros_like(totals[:1]), totals[:-1]], 0)


def attend(query_feat, key_feat, extended, masks):
    carry_keep, row_gate, chosen, block_mask = masks
    nblocks, span_len = row_gate.shape
    head_count = query_feat.shape[1]
    block_q = query_feat.reshape(nblocks, span_len, head_count, -1)
    block_k = key_feat.reshape(nblocks, span_len, head_count, -1)
    block_v = extended.reshape(nblocks, span_len, head_count, -1)
    scores = (
        jnp.einsum("bthj,bshj->bhts", block_q, block_k, precision=highest) * block_mask[:, None]
    )
    inside = jnp.einsum("bhts,bshe->bthe", scores, block_v, precision=highest)
    states = block_states(carry_keep, block_k * chosen[:, :, None, None], block_v)
    outside = jnp.einsum(
        "bthj,bhje->bthe", block_q * row_gate[:, :, None, None], states, precision=highest
    )
    return (inside + outside).reshape(nblocks * span_len, head_count, -1)


def attend_back(query_feat, key_feat, extended, masks, upstream):
    carry_keep, row_gate, chosen, block_mask = masks
    nblocks, span_len = row_gate.shape
    head_count = query_feat.shape[1]
    block_q = query_feat.reshape(nblocks, span_len, head_count, -1)
    block_k = key_feat.reshape(nblocks, span_len, head_count, -1)
    block_v = extended.reshape(nblocks, span_len, head_count, -1)
    block_g = upstream.reshape(nblocks, span_len, head_count, -1)
    picked = block_k * chosen[:, :, None, None]
    gated = block_q * row_gate[:, :, None, None]
    scores = (
        jnp.einsum("bthj,bshj->bhts", block_q, block_k, precision=highest) * block_mask[:, None]
    )
    states = block_states(carry_keep, picked, block_v)
    score_grad = (
        jnp.einsum("bthe,bshe->bhts", block_g, block_v, precision=highest) * block_mask[:, None]
    )
    query_grad = jnp.einsum("bhts,bshj->bthj", score_grad, block_k, precision=highest)
    query_grad = query_grad + row_gate[:, :, None, None] * jnp.einsum(
        "bthe,bhje->bthj", block_g, states, precision=highest
    )
    key_grad = jnp.einsum("bhts,bthj->bshj", score_grad, block_q, precision=highest)
    value_grad = jnp.einsum("bhts,bthe->bshe", scores, block_g, precision=highest)
    state_grad = jnp.einsum("bthj,bthe->bhje", gated, block_g, precision=highest)
    later_total = jnp.flip(carry_chain(jnp.flip(carry_keep, 0), jnp.flip(state_grad, 0)), 0)
    incr_grad = jnp.concatenate([later_total[1:], jnp.zeros_like(later_total[:1])], 0)
    key_grad = key_grad + chosen[:, :, None, None] * jnp.einsum(
        "bhje,bshe->bshj", incr_grad, block_v, precision=highest
    )
    value_grad = value_grad + jnp.einsum("bshj,bhje->bshe", picked, incr_grad, precision=highest)
    row_total = nblocks * span_len
    return (
        query_grad.reshape(row_total, head_count, -1),
        key_grad.reshape(row_total, head_count, -1),
        value_grad.reshape(row_total, head_count, -1),
    )


def on_device(
    tokens,
    doc_lengths,
    norm_gain,
    norm_shift,
    qkv_weight,
    qkv_bias,
    omega,
    qmc_weights,
    out_weight,
    out_bias,
    up_weight,
    up_bias,
    down_weight,
    out_grad,
):
    feat_parts = lax.axis_size("feat")
    feat_index = lax.axis_index("feat")
    qkv_full, up_full, out_rows, down_rows = (
        lax.all_gather(qkv_weight, "dp", axis=0, tiled=True),
        lax.all_gather(up_weight, "dp", axis=0, tiled=True),
        lax.all_gather(out_weight, "dp", axis=1, tiled=True),
        lax.all_gather(down_weight, "dp", axis=1, tiled=True),
    )
    gain_vec = norm_gain.astype(jnp.float32)
    shift_vec = norm_shift.astype(jnp.float32)
    inputs = tokens.astype(jnp.float32)
    row_sums = lax.psum((jnp.sum(inputs, 1), jnp.sum(inputs * inputs, 1)), "feat")
    center = row_sums[0] / D
    spread = row_sums[1] / D - center * center
    inv_root = lax.rsqrt(spread + epsilon)
    standard = (inputs - center[:, None]) * inv_root[:, None]
    normed_all = lax.all_gather(
        (standard * gain_vec + shift_vec).astype(jnp.bfloat16), "feat", axis=1, tiled=True
    )
    local_width = tokens.shape[1]
    local_heads = local_width // HD
    feat_count = M // feat_parts
    omega_used = lax.dynamic_slice_in_dim(omega, feat_index * feat_count, feat_count, 1)
    weights_used = lax.dynamic_slice_in_dim(qmc_weights, feat_index * feat_count, feat_count, 0)
    row_count = tokens.shape[0] // MB
    qkv_bias_f = qkv_bias.astype(jnp.float32)
    up_bias_f = up_bias.astype(jnp.float32)
    out_bias_f = out_bias.astype(jnp.float32)
    block_outs = []
    saved_state = []
    for micro_idx in range(MB):
        offset = micro_idx * row_count
        normed_rows = normed_all[offset : offset + row_count]
        segment, positions = row_layout(doc_lengths[micro_idx], row_count)
        masks = block_masks(segment)
        projected = (
            jnp.einsum("rd,dcf->rcf", normed_rows, qkv_full, preferred_element_type=jnp.float32)
            + qkv_bias_f
        ).astype(jnp.bfloat16)
        pre_act = jnp.dot(normed_rows, up_full, preferred_element_type=jnp.float32) + up_bias_f
        hidden = gelu_exact(pre_act).astype(jnp.bfloat16)
        projected_used = lax.all_gather(projected, "feat", axis=2, tiled=True)
        heads_used = projected_used.shape[2] // HD
        heads_view = projected_used.astype(jnp.float32).reshape(row_count, 3, heads_used, HD)
        queries = heads_view[:, 0]
        keys_raw = heads_view[:, 1]
        query_map, key_map = both_maps(queries, keys_raw, positions, omega_used, weights_used)
        query_feat = query_map.astype(jnp.bfloat16).astype(jnp.float32)
        key_feat = key_map.astype(jnp.bfloat16).astype(jnp.float32)
        extended = jnp.concatenate(
            [heads_view[:, 2], jnp.ones((row_count, heads_used, 1), jnp.float32)], 2
        )
        mixed = attend(query_feat, key_feat, extended, masks)
        numerator = mixed[..., :HD]
        denominator = mixed[..., HD]
        numerator, denominator = (
            lax.psum_scatter(numerator, "feat", scatter_dimension=1, tiled=True),
            lax.psum_scatter(denominator, "feat", scatter_dimension=1, tiled=True),
        )
        attended = (
            (numerator / denominator[..., None])
            .reshape(row_count, local_width)
            .astype(jnp.bfloat16)
        )
        branch = jnp.dot(attended, out_rows, preferred_element_type=jnp.float32)
        branch = branch + jnp.dot(hidden, down_rows, preferred_element_type=jnp.float32)
        summed = lax.psum_scatter(
            branch.astype(jnp.bfloat16), "feat", scatter_dimension=1, tiled=True
        ).astype(jnp.float32)
        block_outs.append(
            (inputs[offset : offset + row_count] + summed + out_bias_f).astype(jnp.bfloat16)
        )
        saved_state.append(
            (
                normed_rows,
                positions,
                masks,
                pre_act,
                hidden,
                queries,
                keys_raw,
                extended,
                query_feat,
                key_feat,
                numerator,
                denominator,
                attended,
            )
        )
    qkv_acc = jnp.zeros(qkv_full.shape, jnp.float32)
    up_acc = jnp.zeros(up_full.shape, jnp.float32)
    outw_acc = jnp.zeros(out_rows.shape, jnp.float32)
    down_acc = jnp.zeros(down_rows.shape, jnp.float32)
    qkv_bias_acc = jnp.zeros((3, local_width), jnp.float32)
    up_bias_acc = jnp.zeros((up_full.shape[1],), jnp.float32)
    normed_grads = []
    for micro_idx in range(MB):
        offset = micro_idx * row_count
        (
            normed_rows,
            positions,
            masks,
            pre_act,
            hidden,
            queries,
            keys_raw,
            extended,
            query_feat,
            key_feat,
            numerator,
            denominator,
            attended,
        ) = saved_state[micro_idx]
        cotangent = lax.all_gather(
            out_grad[offset : offset + row_count], "feat", axis=1, tiled=True
        )
        outw_acc = outw_acc + jnp.einsum(
            "rk,rd->kd", attended, cotangent, preferred_element_type=jnp.float32
        )
        down_acc = down_acc + jnp.einsum(
            "rk,rd->kd", hidden, cotangent, preferred_element_type=jnp.float32
        )
        att_grad = jnp.einsum("rd,kd->rk", cotangent, out_rows, preferred_element_type=jnp.float32)
        hidden_grad = jnp.einsum(
            "rd,kd->rk", cotangent, down_rows, preferred_element_type=jnp.float32
        )
        _, gelu_pull = jax.vjp(gelu_exact, pre_act)
        pre_grad = gelu_pull(hidden_grad)[0].astype(jnp.bfloat16)
        up_acc = up_acc + jnp.einsum(
            "rd,rk->dk", normed_rows, pre_grad, preferred_element_type=jnp.float32
        )
        up_bias_acc = up_bias_acc + jnp.sum(pre_grad.astype(jnp.float32), 0)
        att_grad = att_grad.reshape(row_count, local_heads, HD)
        numer_grad = (att_grad / denominator[..., None]).astype(jnp.bfloat16)
        denom_grad = (-jnp.sum(att_grad * numerator, 2) / (denominator * denominator)).astype(
            jnp.bfloat16
        )
        numer_grad, denom_grad = (
            lax.all_gather(numer_grad, "feat", axis=1, tiled=True),
            lax.all_gather(denom_grad, "feat", axis=1, tiled=True),
        )
        upstream = jnp.concatenate(
            [numer_grad.astype(jnp.float32), denom_grad.astype(jnp.float32)[..., None]], 2
        )
        query_feat_grad, key_feat_grad, extended_grad = attend_back(
            query_feat, key_feat, extended, masks, upstream
        )

        def map_local(query_in, key_in):
            return both_maps(query_in, key_in, positions, omega_used, weights_used)

        _, map_pull = jax.vjp(map_local, queries, keys_raw)
        query_grad, key_grad = map_pull((query_feat_grad, key_feat_grad))
        proj_rows = jnp.stack([query_grad, key_grad, extended_grad[..., :HD]], 1).reshape(
            row_count, 3, -1
        )
        proj_rows = lax.psum_scatter(proj_rows, "feat", scatter_dimension=2, tiled=True)
        proj_grad = proj_rows.astype(jnp.bfloat16)
        qkv_acc = qkv_acc + jnp.einsum(
            "rd,rcf->dcf", normed_rows, proj_grad, preferred_element_type=jnp.float32
        )
        qkv_bias_acc = qkv_bias_acc + jnp.sum(proj_grad.astype(jnp.float32), 0)
        normed_part = jnp.einsum(
            "rcf,dcf->rd", proj_grad, qkv_full, preferred_element_type=jnp.float32
        )
        normed_part = normed_part + jnp.einsum(
            "rk,dk->rd", pre_grad, up_full, preferred_element_type=jnp.float32
        )
        normed_grads.append(
            lax.psum_scatter(
                normed_part.astype(jnp.bfloat16), "feat", scatter_dimension=1, tiled=True
            ).astype(jnp.float32)
        )
    normed_grad = jnp.concatenate(normed_grads, 0)
    scaled = normed_grad * gain_vec
    grad_sums = lax.psum((jnp.sum(scaled, 1), jnp.sum(scaled * standard, 1)), "feat")
    out_grad_f = out_grad.astype(jnp.float32)
    input_grad = out_grad_f + inv_root[:, None] * (
        scaled - grad_sums[0][:, None] / D - standard * grad_sums[1][:, None] / D
    )
    gain_part = jnp.sum(normed_grad * standard, 0)
    shift_part = jnp.sum(normed_grad, 0)
    out_bias_part = jnp.sum(out_grad_f, 0)
    qkv_grad, up_grad, outw_grad, down_grad = (
        lax.psum_scatter(
            qkv_acc.astype(jnp.bfloat16), "dp", scatter_dimension=0, tiled=True
        ).astype(jnp.float32),
        lax.psum_scatter(up_acc.astype(jnp.bfloat16), "dp", scatter_dimension=0, tiled=True).astype(
            jnp.float32
        ),
        lax.psum_scatter(
            outw_acc.astype(jnp.bfloat16), "dp", scatter_dimension=1, tiled=True
        ).astype(jnp.float32),
        lax.psum_scatter(
            down_acc.astype(jnp.bfloat16), "dp", scatter_dimension=1, tiled=True
        ).astype(jnp.float32),
    )
    gain_grad, shift_grad, qkv_bias_grad, out_bias_grad, up_bias_grad = lax.psum(
        (gain_part, shift_part, qkv_bias_acc, out_bias_part, up_bias_acc), "dp"
    )
    return (
        jnp.concatenate(block_outs, 0),
        input_grad.astype(jnp.bfloat16),
        gain_grad,
        shift_grad,
        qkv_grad,
        qkv_bias_grad,
        outw_grad,
        out_bias_grad,
        up_grad,
        up_bias_grad,
        down_grad,
    )


def solution(mesh):
    in_specs = (
        P("dp", "feat"),
        P("dp", None),
        P("feat"),
        P("feat"),
        P("dp", None, "feat"),
        P(None, "feat"),
        P(),
        P(),
        P("feat", "dp"),
        P("feat"),
        P("dp", "feat"),
        P("feat"),
        P("feat", "dp"),
        P("dp", "feat"),
    )
    out_specs = (
        P("dp", "feat"),
        P("dp", "feat"),
        P("feat"),
        P("feat"),
        P("dp", None, "feat"),
        P(None, "feat"),
        P("feat", "dp"),
        P("feat"),
        P("dp", "feat"),
        P("feat"),
        P("feat", "dp"),
    )
    return jax.shard_map(
        on_device, mesh=mesh, in_specs=in_specs, out_specs=out_specs, check_vma=False
    )
```

profile of v0, /device:TPU:0, one launch (start us, length us, event | category | flops | bytes accessed | tf_op | source)
XLA Modules:
  0.0 946.7 jit_solution(9523715599938888410)
XLA Ops:
  9.7 8.4 all-reduce.39
  21.5 15.8 %all-gather.9.cloned.1.call-done = bf16[512,1024]{1,0:T(8,128)(2,1)} async-done(((bf16[512,256]{1,0:T(8,128)(2,1)}), bf16[512,1024]{1,0:T(8,128)(2,1)}) %all-gather.9.cloned.1.call-update) | async-done | bytes 1048592 | tf_op jit(solution)/shard_map/all_gather | solution.py:193
  37.3 46.4 %all-gather.11.cloned.1.call-done = bf16[1024,3,256]{2,0,1:T(8,128)(2,1)} async-done(((bf16[128,3,256]{2,0,1:T(8,128)(2,1)}), bf16[1024,3,256]{2,0,1:T(8,128)(2,1)}) %all-gather.11.cloned.1.call-update) | async-done | bytes 1572880 | tf_op jit(solution)/shard_map/all_gather | solution.py:180
  83.7 3.0 fusion.30
  95.5 9.6 %all-gather.19.cloned.1.call-done = bf16[256,3,1024]{2,0,1:T(8,128)(2,1)} async-done(((bf16[256,3,256]{2,0,1:T(8,128)(2,1)}), bf16[256,3,1024]{2,0,1:T(8,128)(2,1)}) %all-gather.19.cloned.1.call-update) | async-done | bytes 1572880 | tf_op jit(solution)/shard_map/all_gather | solution.py:218
  113.7 13.3 %all-gather.13.cloned.1.call-done = bf16[256,3,1024]{2,0,1:T(8,128)(2,1)} async-done(((bf16[256,3,256]{2,0,1:T(8,128)(2,1)}), bf16[256,3,1024]{2,0,1:T(8,128)(2,1)}) %all-gather.13.cloned.1.call-update) | async-done | bytes 1572880 | tf_op jit(solution)/shard_map/all_gather | solution.py:218
  136.9 2.4 reshape.592
  139.3 3.0 copy.250
  147.0 2.8 multiply_convert_fusion.3
  149.9 2.4 concatenate.110
  152.4 3.5 reshape.591
  155.9 4.0 copy.238
  166.0 15.1 %pad.399 = f32[4,16,16,65]{3,2,1,0:T(8,128)} pad(f32[2,16,16,65]{3,2,1,0:T(8,128)} %pad_add_fusion.7, f32[]{:T(128)} %constant.45.clone.1), padding=1_0_1x0_0_0x0_0_0x0_0_0 | pad | bytes 399364
  182.5 4.6 fusion.93
  187.1 5.3 add_bitcast_fusion.3
  192.5 4.1 copy.242
  196.6 3.3 reshape.544
  206.5 15.2 %pad.398 = f32[4,16,16,65]{3,2,1,0:T(8,128)} pad(f32[2,16,16,65]{3,2,1,0:T(8,128)} %pad_add_fusion.6, f32[]{:T(128)} %constant.45.clone.1), padding=1_0_1x0_0_0x0_0_0x0_0_0 | pad | bytes 399364
  223.2 3.4 fusion.90
  226.7 3.7 add_bitcast_fusion.2
  230.3 4.1 copy.254
  234.5 3.2 reshape.554
  245.7 7.6 all_gather.46
  253.4 27.3 %all_gather.42 = bf16[256,1024]{1,0:T(8,128)(2,1)S(1)} all-gather(bf16[256,128]{1,0:T(8,128)(2,1)S(1)} %copy-done.111), channel_id=1, replica_groups=mesh['dp'=8,'feat'=4] {'dp'}, dimensions={1}, use_global_device_ids=true | all-gather | bytes 589824 | tf_op jit(solution)/shard_map/all_gather | solution.py:182
  281.4 6.5 all_gather.49
  291.2 12.2 %all-reduce.38 = (f32[256,16]{0,1:T(8,128)S(1)}, f32[256,16]{0,1:T(8,128)S(1)}) all-reduce(f32[256,16]{0,1:T(8,128)S(1)} %slice_bitcast_fusion.6, f32[256,16]{0,1:T(8,128)S(1)} %slice_bitcast_fusion.7), channel_id=6, replica_groups=mesh['dp'=8,'feat'=4] {'feat'}, use_global_device_ids=true, to_apply=%region_18.19.clone | all-reduce | flops 8192 | bytes 65536
  306.6 7.0 all_gather.47
  313.5 2.8 concatenate.127
  316.3 2.4 copy.256
  318.7 5.2 all-gather
  328.8 3.1 fusion.261
  334.2 15.1 %pad.401 = f32[4,16,16,65]{3,2,1,0:T(8,128)} pad(f32[2,16,16,65]{3,2,1,0:T(8,128)} %pad_add_fusion.5, f32[]{:T(128)} %constant.45.clone.1), padding=1_0_1x0_0_0x0_0_0x0_0_0 | pad | bytes 399364
  351.7 15.1 %pad.180 = f32[3,16,16,65]{3,2,1,0:T(8,128)} pad(f32[2,16,16,65]{3,2,1,0:T(8,128)} %pad_maximum_fusion.16, f32[]{:T(128)} %constant.45.clone.1), padding=0_0_1x0_0_0x0_0_0x0_0_0 | pad | bytes 332804 | tf_op jit(solution)/shard_map/slice | solution.py:148
  370.5 5.1 fusion.48
  375.6 2.5 fusion.6
  383.2 7.7 all_gather.50
  394.4 5.3 all-gather.1
  405.3 2.6 fusion.2
  407.9 2.5 fusion.32
  417.9 3.0 fusion.34
  435.3 4.8 add_bitcast_fusion.1
  440.1 4.1 copy.265
  444.3 3.3 reshape.558
  459.5 15.2 %pad.400 = f32[4,16,16,65]{3,2,1,0:T(8,128)} pad(f32[2,16,16,65]{3,2,1,0:T(8,128)} %pad_add_fusion.4, f32[]{:T(128)} %constant.45.clone.1), padding=1_0_1x0_0_0x0_0_0x0_0_0 | pad | bytes 399364
  477.1 15.5 %pad.182 = f32[3,16,16,65]{3,2,1,0:T(8,128)} pad(f32[2,16,16,65]{3,2,1,0:T(8,128)} %pad_maximum_fusion.17, f32[]{:T(128)} %constant.45.clone.1), padding=0_0_1x0_0_0x0_0_0x0_0_0 | pad | bytes 332804 | tf_op jit(solution)/shard_map/slice | solution.py:148
  496.3 4.5 fusion.47
  505.6 2.4 fusion.21
  513.8 5.0 add_bitcast_fusion
  518.7 3.3 copy.277
  531.6 5.9 convert_reduce_fusion
  540.9 4.0 convert_reduce_fusion.1
  548.8 3.9 copy.304
  565.5 2.4 convolution_bitcast_fusion.1
  569.6 2.3 convolution_bitcast_fusion
  578.2 59.0 %reduce-scatter.39.cloned.1.call-done = bf16[128,1024]{1,0:T(8,128)(2,1)} async-done(((bf16[1024,1024]{1,0:T(8,128)(2,1)}), bf16[128,1024]{1,0:T(8,128)(2,1)}) %reduce-scatter.39.cloned.1.call-update) | async-done | bytes 262160
  639.1 69.0 %reduce-scatter.35.cloned.1.call-done = bf16[128,1024]{1,0:T(8,128)(2,1)} async-done(((bf16[1024,1024]{1,0:T(8,128)(2,1)}), bf16[128,1024]{1,0:T(8,128)(2,1)}) %reduce-scatter.35.cloned.1.call-update) | async-done | bytes 262160 | tf_op jit(solution)/shard_map/reduce_scatter | solution.py:364
  709.9 63.2 %reduce-scatter.37.cloned.1.call-done = bf16[128,256]{1,0:T(8,128)(2,1)} async-done(((bf16[1024,256]{1,0:T(8,128)(2,1)}), bf16[128,256]{1,0:T(8,128)(2,1)}) %reduce-scatter.37.cloned.1.call-update) | async-done | bytes 65552
  774.7 21.4 %reduce-scatter.23.cloned.1.call-done = bf16[256,256]{1,0:T(8,128)(2,1)} async-done(((bf16[256,1024]{1,0:T(8,128)(2,1)}), bf16[256,256]{1,0:T(8,128)(2,1)}) %reduce-scatter.23.cloned.1.call-update) | async-done | bytes 131088 | tf_op jit(solution)/shard_map/reduce_scatter | solution.py:243
  796.2 24.1 %reduce-scatter.19.cloned.1.call-done = bf16[256,256]{1,0:T(8,128)(2,1)} async-done(((bf16[256,1024]{1,0:T(8,128)(2,1)}), bf16[256,256]{1,0:T(8,128)(2,1)}) %reduce-scatter.19.cloned.1.call-update) | async-done | bytes 131088 | tf_op jit(solution)/shard_map/reduce_scatter | solution.py:243
  822.4 21.9 %reduce-scatter.27.cloned.1.call-done = bf16[256,256]{1,0:T(8,128)(2,1)} async-done(((bf16[256,1024]{1,0:T(8,128)(2,1)}), bf16[256,256]{1,0:T(8,128)(2,1)}) %reduce-scatter.27.cloned.1.call-update) | async-done | bytes 131088 | tf_op jit(solution)/shard_map/reduce_scatter | solution.py:346
  845.2 23.1 %reduce-scatter.31.cloned.1.call-done = bf16[256,256]{1,0:T(8,128)(2,1)} async-done(((bf16[256,1024]{1,0:T(8,128)(2,1)}), bf16[256,256]{1,0:T(8,128)(2,1)}) %reduce-scatter.31.cloned.1.call-update) | async-done | bytes 131088 | tf_op jit(solution)/shard_map/reduce_scatter | solution.py:346
  871.5 5.8 all-reduce.37
  878.3 37.3 %all-reduce.36 = (f32[256]{0:T(256)}, f32[256]{0:T(256)}, f32[3,256]{1,0:T(4,128)}, f32[256]{0:T(256)}, f32[1024]{0:T(1024)}) all-reduce(f32[256]{0:T(256)S(1)} %get-tuple-element.11, f32[256]{0:T(256)S(1)} %reduce_sum.286, f32[3,256]{1,0:T(4,128)S(1)} %add.431, ...), channel_id=1, replica_groups=mesh['dp'=8,'feat'=4] {'dp'}, use_global_device_ids=true, to_apply=%region_35.36 | all-reduce | flops 2560 | bytes 20480 | tf_op jit(solution)/shard_map/psum | solution.py:374
  915.6 22.1 %reduce-scatter.33.cloned.1.call-done = bf16[128,3,256]{2,0,1:T(8,128)(2,1)} async-done(((bf16[1024,3,256]{2,0,1:T(8,128)(2,1)}), bf16[128,3,256]{2,0,1:T(8,128)(2,1)}) %reduce-scatter.33.cloned.1.call-update) | async-done | bytes 196624 | tf_op jit(solution)/shard_map/reduce_scatter | solution.py:361
  (558 shorter events, 194.9 us)
Async XLA Ops:
  7.2 128.0 %copy-start = (f32[64,64]{1,0:T(8,128)S(1)}, f32[64,64]{1,0:T(8,128)}, u32[]{:S(2)}) copy-start(f32[64,64]{1,0:T(8,128)} %param.20) | copy-start | bytes 49156
  7.2 30.1 %all-gather.9.cloned.1.call-start = ((), (), s32[]{:S(2)}) async-start(), calls=%async_computation.12 | async-start | bytes 1310720 | tf_op jit(solution)/shard_map/all_gather | solution.py:193
  9.1 28.2 %copy-start.120 = (f32[256]{0:T(256)}, f32[256]{0:T(256)S(1)}, u32[]{:S(2)}) copy-start(f32[256]{0:T(256)S(1)} %convert_element_type.248) | copy-start | bytes 3076
  18.1 68.7 %copy-start.124 = (s32[2,3]{1,0:T(2,128)S(1)}, s32[2,3]{1,0:T(2,128)}, u32[]{:S(2)}) copy-start(s32[2,3]{1,0:T(2,128)} %param.15) | copy-start | bytes 76
  20.0 63.7 %all-gather.11.cloned.1.call-start = ((), (), s32[]{:S(2)}) async-start(), calls=%async_computation.13 | async-start | bytes 1769472 | tf_op jit(solution)/shard_map/all_gather | solution.py:180
  20.8 84.4 %all-gather.19.cloned.1.call-start = ((), (), s32[]{:S(2)}) async-start(), calls=%async_computation.19 | async-start | bytes 1966080 | tf_op jit(solution)/shard_map/all_gather | solution.py:218
  37.3 51.0 %copy-start.44 = (bf16[512,1024]{1,0:T(8,128)(2,1)S(1)}, bf16[512,1024]{1,0:T(8,128)(2,1)}, u32[]{:S(2)}) copy-start(bf16[512,1024]{1,0:T(8,128)(2,1)} %all-gather.9.cloned.1.call-done) | copy-start | bytes 3145732
  83.7 4.7 copy-start.43
  86.7 7.1 copy-start.136
  86.7 40.2 %all-gather.13.cloned.1.call-start = ((), (), s32[]{:S(2)}) async-start(), calls=%async_computation.14 | async-start | bytes 1966080 | tf_op jit(solution)/shard_map/all_gather | solution.py:218
  87.5 45.2 %copy-start.116 = (f32[64]{0:T(128)}, f32[64]{0:T(128)S(1)}, u32[]{:S(2)}) copy-start(f32[64]{0:T(128)S(1)} %get-tuple-element.134) | copy-start | bytes 772
  87.5 45.2 %copy-start.118 = (f32[64]{0:T(128)}, f32[64]{0:T(128)S(1)}, u32[]{:S(2)}) copy-start(f32[64]{0:T(128)S(1)} %get-tuple-element.135) | copy-start | bytes 772
  88.2 6.1 copy-start.126
  88.2 18.6 %copy-start.128 = (f32[4]{0:T(128)}, f32[4]{0:T(128)S(1)}, u32[]{:S(2)}) copy-start(f32[4]{0:T(128)S(1)} %get-tuple-element.129) | copy-start | bytes 52
  89.7 213.7 %reduce-scatter.17.cloned.1.call-start = ((), (), s32[]{:S(2)}) async-start(), calls=%async_computation.15 | async-start | bytes 1310720 | tf_op jit(solution)/shard_map/reduce_scatter | solution.py:233
  89.8 17.0 %copy-start.129 = (f32[2]{0:T(128)}, f32[2]{0:T(128)S(1)}, u32[]{:S(2)}) copy-start(f32[2]{0:T(128)S(1)} %slice.441) | copy-start | bytes 28
  89.9 4.5 copy-start.138
  90.0 4.4 copy-start.132
  90.1 5.4 copy-start.140
  94.5 128.1 %copy-start.112 = (f32[4,64]{1,0:T(4,128)}, f32[4,64]{1,0:T(4,128)S(1)}, u32[]{:S(2)}) copy-start(f32[4,64]{1,0:T(4,128)S(1)} %get-tuple-element.103) | copy-start | bytes 3076
  94.6 87.9 %copy-start.114 = (f32[4,64]{1,0:T(4,128)}, f32[4,64]{1,0:T(4,128)S(1)}, u32[]{:S(2)}) copy-start(f32[4,64]{1,0:T(4,128)S(1)} %get-tuple-element.101) | copy-start | bytes 3076
  130.2 4.8 copy-start.95
  130.2 4.8 copy-start.97
  142.3 4.7 copy-start.122
  144.9 16.8 %copy-start.34 = (bf16[4,64,16,16]{1,0,3,2:T(4,128)(2,1)}, bf16[4,64,16,16]{1,0,3,2:T(4,128)(2,1)S(1)}, u32[]{:S(2)}) copy-start(bf16[4,64,16,16]{1,0,3,2:T(4,128)(2,1)S(1)} %reshape.541) | copy-start | bytes 393220
  149.9 32.6 %copy-start.40 = (bf16[4,64,16,16]{1,0,3,2:T(4,128)(2,1)}, bf16[4,64,16,16]{1,0,3,2:T(4,128)(2,1)S(1)}, u32[]{:S(2)}) copy-start(bf16[4,64,16,16]{1,0,3,2:T(4,128)(2,1)S(1)} %reshape.540) | copy-start | bytes 393220
  181.1 6.0 copy-start.73
  182.5 10.0 %copy-start.66 = (f32[3,16,16,65]{3,2,1,0:T(8,128)}, f32[3,16,16,65]{3,2,1,0:T(8,128)S(1)}, u32[]{:S(2)}) copy-start(f32[3,16,16,65]{3,2,1,0:T(8,128)S(1)} %pad.176) | copy-start | bytes 599044
  182.5 4.6 copy-start.3
  202.7 177.5 %reduce-scatter.21.cloned.1.call-start = ((), (), s32[]{:S(2)}) async-start(), calls=%async_computation.20 | async-start | bytes 1310720 | tf_op jit(solution)/shard_map/reduce_scatter | solution.py:233
  205.0 17.5 %copy-start.38 = (bf16[4,64,16,16]{1,0,3,2:T(4,128)(2,1)}, bf16[4,64,16,16]{1,0,3,2:T(4,128)(2,1)S(1)}, u32[]{:S(2)}) copy-start(bf16[4,64,16,16]{1,0,3,2:T(4,128)(2,1)S(1)} %reshape.550) | copy-start | bytes 393220
  222.0 4.6 copy-start.68
  238.9 14.4 %copy-start.111 = (bf16[256,128]{1,0:T(8,128)(2,1)S(1)}, bf16[256,128]{1,0:T(8,128)(2,1)}, u32[]{:S(2)}) copy-start(bf16[256,128]{1,0:T(8,128)(2,1)} %param.22) | copy-start | bytes 196612
  240.6 288.1 %all-gather.15.cloned.1.call-start = ((), (), s32[]{:S(2)}) async-start(), calls=%async_computation.16 | async-start | bytes 2359296 | tf_op jit(solution)/shard_map/all_gather | solution.py:181
  241.3 290.2 %all-gather.17.cloned.1.call-start = ((), (), s32[]{:S(2)}) async-start(), calls=%async_computation.17 | async-start | bytes 2359296 | tf_op jit(solution)/shard_map/all_gather | solution.py:183
  242.1 323.5 %reduce-scatter.25.cloned.1.call-start = ((), (), s32[]{:S(2)}) async-start(), calls=%async_computation.22 | async-start | bytes 3932160 | tf_op jit(solution)/shard_map/reduce_scatter | solution.py:333
  242.8 38.6 %copy-start.134 = (f32[2]{0:T(128)}, f32[2]{0:T(128)S(1)}, u32[]{:S(2)}) copy-start(f32[2]{0:T(128)S(1)} %slice.458) | copy-start | bytes 28
  280.7 99.5 %copy-start.14 = (bf16[256,1024]{1,0:T(8,128)(2,1)}, bf16[256,1024]{1,0:T(8,128)(2,1)S(1)}, u32[]{:S(2)}) copy-start(bf16[256,1024]{1,0:T(8,128)(2,1)S(1)} %all_gather.42) | copy-start | bytes 1572868
  287.8 92.3 %copy-start.24 = (bf16[256,1024]{1,0:T(8,128)(2,1)}, bf16[256,1024]{1,0:T(8,128)(2,1)S(1)}, u32[]{:S(2)}) copy-start(bf16[256,1024]{1,0:T(8,128)(2,1)S(1)} %all_gather.49) | copy-start | bytes 1572868
  370.5 5.1 copy-start.10
  370.5 5.2 copy-start.35
  370.5 5.2 copy-start.74
  405.2 5.2 copy-start.8
  410.4 7.5 copy-start.113
  417.9 6.3 copy-start.123
  421.0 6.8 copy-start.117
  421.0 6.8 copy-start.119
  452.6 117.0 %reduce-scatter.29.cloned.1.call-start = ((), (), s32[]{:S(2)}) async-start(), calls=%async_computation.24 | async-start | bytes 3932160 | tf_op jit(solution)/shard_map/reduce_scatter | solution.py:333
  496.2 4.5 copy-start.9
  496.2 4.5 copy-start.39
  496.3 4.5 copy-start.71
  528.0 109.1 %reduce-scatter.39.cloned.1.call-start = ((), (), s32[]{:S(2)}) async-start(), calls=%async_computation.29 | async-start | bytes 2359296
  531.5 6.1 copy-start.46
  539.1 7.7 copy-start.49
  552.8 155.4 %reduce-scatter.35.cloned.1.call-start = ((), (), s32[]{:S(2)}) async-start(), calls=%async_computation.27 | async-start | bytes 2359296 | tf_op jit(solution)/shard_map/reduce_scatter | solution.py:364
  557.0 216.1 %reduce-scatter.37.cloned.1.call-start = ((), (), s32[]{:S(2)}) async-start(), calls=%async_computation.28 | async-start | bytes 589824
  561.4 234.8 %reduce-scatter.23.cloned.1.call-start = ((), (), s32[]{:S(2)}) async-start(), calls=%async_computation.21 | async-start | bytes 655360 | tf_op jit(solution)/shard_map/reduce_scatter | solution.py:243
  563.5 256.7 %reduce-scatter.19.cloned.1.call-start = ((), (), s32[]{:S(2)}) async-start(), calls=%async_computation.18 | async-start | bytes 655360 | tf_op jit(solution)/shard_map/reduce_scatter | solution.py:243
  565.4 278.8 %reduce-scatter.27.cloned.1.call-start = ((), (), s32[]{:S(2)}) async-start(), calls=%async_computation.23 | async-start | bytes 655360 | tf_op jit(solution)/shard_map/reduce_scatter | solution.py:346
  569.5 298.8 %reduce-scatter.31.cloned.1.call-start = ((), (), s32[]{:S(2)}) async-start(), calls=%async_computation.25 | async-start | bytes 655360 | tf_op jit(solution)/shard_map/reduce_scatter | solution.py:346
  573.6 364.2 %reduce-scatter.33.cloned.1.call-start = ((), (), s32[]{:S(2)}) async-start(), calls=%async_computation.26 | async-start | bytes 1769472 | tf_op jit(solution)/shard_map/reduce_scatter | solution.py:361
  774.7 96.4 %copy-start.121 = (f32[256]{0:T(256)S(1)}, f32[256]{0:T(256)}, u32[]{:S(2)}) copy-start(f32[256]{0:T(256)} %copy-done.120) | copy-start | bytes 3076
  821.2 56.0 %copy-start.109 = (bf16[512,256]{1,0:T(8,128)(2,1)S(1)}, bf16[512,256]{1,0:T(8,128)(2,1)}, u32[]{:S(2)}) copy-start(bf16[512,256]{1,0:T(8,128)(2,1)} %param.27) | copy-start | bytes 786436
  822.2 117.3 %copy-start.1 = (f32[64,64]{1,0:T(8,128)S(1)}, f32[64,64]{1,0:T(8,128)}, u32[]{:S(2)}) copy-start(f32[64,64]{1,0:T(8,128)} %param.20) | copy-start | bytes 49156
  (102 other events, 217.9 us)
Sparse Core Ops, SparseCore 0:
  20.1 17.1 all-gather.8
  39.5 44.1 all-gather.10
  86.8 18.2 all-gather.18
  107.1 19.7 all-gather.12
  202.8 24.7 reduce-scatter.16
  240.7 24.7 reduce-scatter.20
  267.6 49.0 all-gather.14
  318.8 48.8 all-gather.16
  452.7 37.0 reduce-scatter.24
  528.1 37.0 reduce-scatter.28
  568.8 68.3 reduce-scatter.38
  640.5 67.5 reduce-scatter.34
  711.5 61.5 reduce-scatter.36
  775.4 20.6 reduce-scatter.22
  798.5 21.6 reduce-scatter.18
  822.5 21.6 reduce-scatter.26
  846.6 21.6 reduce-scatter.30
  871.6 66.0 reduce-scatter.32
where the time goes:
time: 966 us; the launch traced here: 947 us
  waiting for transfers between devices  391 us (40%)
  local copies, waits for them, and re-layouts  215 us (22%)
  matrix products  140 us (14%)
  blocking collectives  130 us (13%)
  other arithmetic  50.4 us (5%)
  between operations  18.7 us (2%)
    unnamed x20, waiting for transfers between devices  124 us
    unnamed x293, local copies, waits for them, and re-layouts  84.1 us
    reduce_scatter x1, waiting for transfers between devices, on_device(): lax.psum_scatter(up_acc.astype(jnp.bfloat16), 'dp', scatter_dimension=0,...  69 us
    all_gather x1, waiting for transfers between devices, on_device(): lax.all_gather(qkv_weight, 'dp', axis=0, tiled=True)  46.4 us
    reduce_scatter x2, waiting for transfers between devices, on_device(): lax.psum_scatter(branch.astype(jnp.bfloat16), 'feat', scatter_dimension=1...  45.5 us
    reduce_scatter x2, waiting for transfers between devices, on_device(): lax.psum_scatter(normed_part.astype(jnp.bfloat16), 'feat', scatter_dimens...  45 us
    psum x1, blocking collectives, on_device(): lax.psum((gain_part, shift_part, qkv_bias_acc, out_bias_part, up_bias_acc...  37.3 us
    slice x4, local copies, waits for them, and re-layouts, attend_back(): later_total[1:]  34.1 us
  transfers between devices with their start and end apart: 18, of which 12 were waited for; matrix products, arithmetic and copies ran while one was open for 32% of the time, Pallas kernels for 0%

commit v1 on v0

--- a/solution.py
+++ b/solution.py
@@ -1,8 +1,13 @@
+import functools
 import math
 
 import jax
 import jax.numpy as jnp
+import ml_dtypes
+import numpy as np
 from jax import lax
+from jax.experimental import pallas as pl
+from jax.experimental.pallas import tpu as pltpu
 from jax.sharding import PartitionSpec as P
 
 D = 1024
@@ -11,6 +16,7 @@
 M = 64
 SPAN = 64
 MB = 2
+SEQS = 3
 
 
 epsilon = 1e-05
@@ -389,6 +395,805 @@
     )
 
 
+MESH = pl.DeviceIdType.MESH
+f32, bf16 = jnp.float32, jnp.bfloat16
+NT = ((1,), (1,))
+TN = ((0,), (0,))
+EXTRA = 16
+
+
+def dot(a, b, dims=((1,), (0,)), precision=None):
+    return lax.dot_general(
+        a, b, (dims, ((), ())), precision=precision, preferred_element_type=f32
+    )
+
+
+def rotary_table(longest):
+    half_rot = ROT // 2
+    inv_freq = np.exp(
+        -np.arange(half_rot, dtype=np.float32)
+        * np.float32(2.0 / ROT)
+        * np.float32(math.log(10000.0))
+    ).astype(np.float32)
+    angles = np.arange(longest, dtype=np.float32)[:, None] * inv_freq[None, :]
+    cosine = np.ones((longest, HD), np.float32)
+    sine = np.zeros((longest, HD), np.float32)
+    for part in range(2):
+        cosine[:, part * half_rot : (part + 1) * half_rot] = np.cos(angles)
+        sine[:, part * half_rot : (part + 1) * half_rot] = np.sin(angles)
+    rest = np.concatenate([cosine, cosine, sine, sine], 1).astype(np.float32)
+    terms = []
+    for _ in range(3):
+        term = rest.astype(ml_dtypes.bfloat16)
+        terms.append(term)
+        rest = rest - term.astype(np.float32)
+    return np.concatenate(terms, 0)
+
+
+def rotary_swap():
+    half_rot = ROT // 2
+    one = np.zeros((HD, HD), np.float32)
+    for i in range(half_rot):
+        one[i + half_rot, i] = -1.0
+        one[i, i + half_rot] = 1.0
+    return np.kron(np.eye(4, dtype=np.float32), one).astype(ml_dtypes.bfloat16)
+
+
+def dct_rows():
+    ramp = np.arange(HD, dtype=np.float32)
+    scale = np.where(ramp == 0.0, np.sqrt(1.0 / HD), np.sqrt(2.0 / HD))
+    table = np.cos(math.pi * (2.0 * ramp[None, :] + 1.0) * ramp[:, None] / (2.0 * HD)) * scale[:, None]
+    return np.tile(table.T, (4, 1)).astype(np.float32)
+
+
+class Sizes:
+    def __init__(self, rows, width, hidden, dp_count, feat_count):
+        self.rows = rows
+        self.width = width
+        self.model = width * feat_count
+        self.span = rows // MB
+        self.total = 2 * rows
+        self.micro = 2 * MB
+        self.half = width // 2
+        self.hidden = hidden // 2
+        self.block = self.model // dp_count
+        self.planes = dp_count // 2
+
+
+def scratch_list(s):
+    pl_, bl, hf, hd, tt, md = s.planes, s.block, s.half, s.hidden, s.total, s.model
+    grads = {
+        "qkv": (3, bl, hf),
+        "out": (hf, bl),
+        "up": (bl, hd),
+        "down": (hd, bl),
+    }
+    shapes = dict(
+        XG=((2, s.rows + EXTRA, md), bf16),
+        G=((tt, md), bf16),
+        WQ=((3, md, hf), bf16),
+        WU=((md, hd), bf16),
+        WO=((hf, md), bf16),
+        WD=((hd, md), bf16),
+        NB=((tt, md), bf16),
+        MU=((tt, 1), f32),
+        IV=((tt, 1), f32),
+        A2=((2 * s.width // 2, s.width), f32),
+        WB=((tt, 2 * hf), bf16),
+        VB=((tt, hf), bf16),
+        PHF=((tt, 2 * hf), f32),
+        PHB=((tt, 2 * hf), bf16),
+        ROTV=((tt, 2 * hf), f32),
+        CSB=((tt, 2 * hf), f32),
+        SB=((s.micro, 2, s.span, s.span), bf16),
+        ND=((tt, 2 * hf), f32),
+        AT=((tt, hf), bf16),
+        PG=((tt, 3 * hf), bf16),
+        HB=((tt, hd), bf16),
+        GP=((tt, hd), f32),
+        PRE=((tt, hd), bf16),
+        QBG=((1, 3 * hf), f32),
+        UBG=((1, hd), f32),
+        NGF=((s.rows, s.width), f32),
+        ST=((16, s.rows), f32),
+        STR=((3, 16, s.rows), f32),
+        SV=((24, 128), f32),
+        SVR=((7, 24, 128), f32),
+    )
+    for name, shape in grads.items():
+        shapes["SX" + name] = ((pl_,) + shape, bf16)
+        shapes["RX" + name] = ((pl_,) + shape, bf16)
+        shapes["KX" + name] = ((pl_,) + shape, f32)
+        shapes["ZS" + name] = ((3,) + shape, bf16)
+        shapes["ZR" + name] = ((3,) + shape, bf16)
+    for name in ("blk", "nrm"):
+        shapes["CS" + name] = ((tt, 2 * s.width), bf16)
+        shapes["CR" + name] = ((tt, 2 * s.width), bf16)
+        shapes["KC" + name] = ((tt, 2 * s.width), f32)
+        shapes["KY" + name] = ((tt, s.width), f32)
+        shapes["YS" + name] = ((tt, s.width), bf16)
+        shapes["YR" + name] = ((tt, s.width), bf16)
+        shapes["AS" + name] = ((s.rows, s.width), bf16)
+        shapes["AR" + name] = ((s.rows, s.width), bf16)
+    return shapes
+
+
+N_LOCAL = 7
+N_REMOTE = 120
+
+
+def fused_kernel(s, names, *refs):
+    (tok, grd, ext, wq_in, wu_in, wo_in, wd_in, small, tab, swap, ones16, dct, rep, omega) = refs[:14]
+    o_blk, o_inp, o_qkv, o_up, o_out, o_down, o_small = refs[14:21]
+    m_ = dict(zip(names, refs[21:]))
+    lsem, ssem, rsem = m_["lsem"], m_["ssem"], m_["rsem"]
+    XG, G, WQ, WU, WO, WD = (m_[k] for k in ("XG", "G", "WQ", "WU", "WO", "WD"))
+    NB, MU, IV = m_["NB"], m_["MU"], m_["IV"]
+
+    dp = lax.axis_index("dp")
+    ft = lax.axis_index("feat")
+    z, x = dp // 2, dp % 2
+    zl = z % 2
+    y, c = ft // 2, ft % 2
+    zd = (z, z + 1 - 2 * zl, z + 2 - 4 * (z // 2), 3 - z)
+    zd = (z, z + 1 - 2 * zl, (z + 2) % 4, z + 1 - 2 * zl + 2 - 4 * (z // 2))
+    hl = (zl, 1 - zl, zl, 1 - zl)
+    counter = [0]
+
+    def new(n=1):
+        counter[0] += n
+        return counter[0] - n
+
+    def device(d=0, fx=False, fy=False, fc=False):
+        return {
+            "dp": zd[d] * 2 + (1 - x if fx else x),
+            "feat": (1 - y if fy else y) * 2 + (1 - c if fc else c),
+        }
+
+    def send(src, dst, sem, where):
+        copy = pltpu.make_async_remote_copy(
+            src_ref=src,
+            dst_ref=dst,
+            send_sem=ssem.at[sem],
+            recv_sem=rsem.at[sem],
+            device_id=where,
+            device_id_type=MESH,
+        )
+        return copy
+
+    sent = []
+
+    def go(src, dst, sem, where):
+        copy = send(src, dst, sem, where)
+        copy.start()
+        sent.append(copy)
+
+    def arrived(ref, sem, where):
+        send(ref, ref, sem, where).wait_recv()
+
+    mo = pl.multiple_of
+
+    def lanes(index, size):
+        return pl.ds(mo(index * size, size), size)
+
+    def tok_at(b, f):
+        return XG.at[b, :, lanes(f, s.width)]
+
+    def grd_at(b, f):
+        return G.at[lanes(b, s.rows), lanes(f, s.width)]
+
+    def own_half(w, h):
+        if w == "qkv":
+            return wq_in.at[:, :, lanes(h, s.half)]
+        if w == "up":
+            return wu_in.at[:, lanes(h, s.hidden)]
+        if w == "out":
+            return wo_in.at[lanes(h, s.half), :]
+        return wd_in.at[lanes(h, s.hidden), :]
+
+    def weight_at(w, block):
+        if w == "qkv":
+            return WQ.at[:, lanes(block, s.block), :]
+        if w == "up":
+            return WU.at[lanes(block, s.block), :]
+        if w == "out":
+            return WO.at[:, lanes(block, s.block)]
+        return WD.at[:, lanes(block, s.block)]
+
+    ws = ("qkv", "out", "up", "down")
+
+    local = [
+        pltpu.make_async_copy(tok, XG.at[zl, pl.ds(0, s.rows), lanes(ft, s.width)], lsem.at[0]),
+        pltpu.make_async_copy(ext, XG.at[zl, pl.ds(s.rows, EXTRA), lanes(ft, s.width)], lsem.at[1]),
+        pltpu.make_async_copy(grd, grd_at(zl, ft), lsem.at[2]),
+    ]
+    for i, w in enumerate(ws):
+        local.append(pltpu.make_async_copy(own_half(w, zl), weight_at(w, dp), lsem.at[3 + i]))
+    for copy in local:
+        copy.start()
+
+    barrier = pltpu.get_barrier_semaphore()
+    partners = [device(d) for d in (1, 2, 3)] + [device(d, fx=True) for d in (0, 1, 2, 3)]
+    partners += [device(fy=True), device(fc=True), device(fy=True, fc=True)]
+    for where in partners:
+        pl.semaphore_signal(barrier, inc=1, device_id=where, device_id_type=MESH)
+    pl.semaphore_wait(barrier, len(partners))
+    for copy in local:
+        copy.wait()
+
+    sem_act = {"tok": new(7), "grd": new(7)}
+
+    def act_first(name, at):
+        base = sem_act[name]
+        go(at(zl, ft), at(zl, ft), base + 1, device(fy=True))
+        go(at(zl, ft), at(zl, ft), base + 2, device(1))
+        go(at(zl, ft), at(zl, ft), base + 0, device(fc=True))
+
+    def act_forward(name, at):
+        base = sem_act[name]
+        fy = (1 - y) * 2 + c
+        zb = 1 - zl
+        arrived(at(zb, ft), base + 2, device(1))
+        go(at(zb, ft), at(zb, ft), base + 3, device(fy=True))
+        go(at(zb, ft), at(zb, ft), base + 4, device(fc=True))
+        arrived(at(zl, fy), base + 1, device(fy=True))
+        go(at(zl, fy), at(zl, fy), base + 5, device(fc=True))
+        arrived(at(zb, fy), base + 3, device(fy=True))
+        go(at(zb, fy), at(zb, fy), base + 6, device(fc=True))
+
+    def act_rest(name, at):
+        base = sem_act[name]
+        fc = y * 2 + 1 - c
+        fyc = (1 - y) * 2 + 1 - c
+        for k, b, f in ((0, zl, fc), (4, 1 - zl, fc), (5, zl, fyc), (6, 1 - zl, fyc)):
+            arrived(at(b, f), base + k, device(fc=True))
+
+    sem_z = {w: new(3) for w in ws}
+    sem_x = {w: new(4) for w in ws}
+
+    def w_z(w):
+        for d in (3, 2, 1):
+            go(own_half(w, hl[d]), weight_at(w, dp), sem_z[w] + d - 1, device(d))
+
+    def w_own(w):
+        go(weight_at(w, dp), weight_at(w, dp), sem_x[w], device(fx=True))
+
+    def w_forward(w, d):
+        block = zd[d] * 2 + x
+        arrived(weight_at(w, block), sem_z[w] + d - 1, device(d))
+        go(weight_at(w, block), weight_at(w, block), sem_x[w] + d, device(fx=True))
+
+    def w_rest(w):
+        for d in range(4):
+            arrived(weight_at(w, zd[d] * 2 + 1 - x), sem_x[w] + d, device(fx=True))
+
+    sem_gx = {w: new(4) for w in ws}
+    sem_gz = {w: new(3) for w in ws}
+
+    def put_grad(w, zp, mine, theirs):
+        m_["KX" + w][zp] = mine
+        m_["SX" + w][zp] = theirs.astype(bf16)
+        src, dst = m_["SX" + w].at[zp], m_["RX" + w].at[zp]
+        send(src, dst, sem_gx[w] + zp, device(fx=True)).start()
+
+    def grad_z(w):
+        for d in (3, 2, 1, 0):
+            zp = zd[d]
+            arrived(m_["RX" + w].at[zp], sem_gx[w] + zp, device(fx=True))
+            both = m_["KX" + w][zp] + m_["RX" + w][zp].astype(f32)
+            if d == 0:
+                m_["KX" + w][zp] = both
+            else:
+                m_["ZS" + w][d - 1] = both.astype(bf16)
+                go(m_["ZS" + w].at[d - 1], m_["ZR" + w].at[d - 1], sem_gz[w] + d - 1, device(d))
+
+    def grad_last(w):
+        for d in (1, 2, 3):
+            arrived(m_["ZR" + w].at[d - 1], sem_gz[w] + d - 1, device(d))
+        got = m_["ZR" + w]
+        same = m_["KX" + w][z] + got[1].astype(f32)
+        other = got[0].astype(f32) + got[2].astype(f32)
+        if w == "qkv":
+            o_qkv[:, :, lanes(zl, s.half)] = same
+            o_qkv[:, :, lanes(1 - zl, s.half)] = other
+        elif w == "up":
+            o_up[:, lanes(zl, s.hidden)] = same
+            o_up[:, lanes(1 - zl, s.hidden)] = other
+        elif w == "out":
+            o_out[lanes(zl, s.half), :] = same
+            o_out[lanes(1 - zl, s.half), :] = other
+        else:
+            o_down[lanes(zl, s.hidden), :] = same
+            o_down[lanes(1 - zl, s.hidden), :] = other
+        for zp in range(4):
+            send(m_["SX" + w].at[zp], m_["RX" + w].at[zp], sem_gx[w] + zp, device(fx=True)).wait_send()
+
+    def pick(flag, a, b):
+        return jnp.where(flag == 0, a, b)
+
+    def halves(value, axis):
+        n = value.shape[axis] // 2
+        lo, hi = lax.slice_in_dim(value, 0, n, axis=axis), lax.slice_in_dim(value, n, 2 * n, axis=axis)
+        return pick(x, lo, hi), pick(x, hi, lo)
+
+    sem_c = {k: new(4) for k in ("blk", "nrm")}
+    sem_y = {k: new(4) for k in ("blk", "nrm")}
+    sem_a = {k: new(2) for k in ("blk", "nrm")}
+
+    def rows_of(i):
+        block = (1 - zl) + (i // MB) * (2 * zl - 1)
+        return pl.ds(mo(block * s.rows + (i % MB) * s.span, s.span), s.span)
+
+    def act_put(name, i, value):
+        r = rows_of(i)
+        w_ = s.width
+        v = [value[:, k * w_ : (k + 1) * w_] for k in range(4)]
+        m_["KC" + name][r, 0:w_] = pick(c, v[0], v[1])
+        m_["KC" + name][r, w_ : 2 * w_] = pick(c, v[2], v[3])
+        m_["CS" + name][r, 0:w_] = pick(c, v[1], v[0]).astype(bf16)
+        m_["CS" + name][r, w_ : 2 * w_] = pick(c, v[3], v[2]).astype(bf16)
+        send(m_["CS" + name].at[r], m_["CR" + name].at[r], sem_c[name] + i, device(fc=True)).start()
+
+    def act_y(name, i):
+        r = rows_of(i)
+        w_ = s.width
+        arrived(m_["CR" + name].at[r], sem_c[name] + i, device(fc=True))
+        both = m_["KC" + name][r, :] + m_["CR" + name][r, :].astype(f32)
+        lo, hi = both[:, :w_], both[:, w_:]
+        m_["KY" + name][r, :] = pick(y, lo, hi)
+        m_["YS" + name][r, :] = pick(y, hi, lo).astype(bf16)
+        send(m_["YS" + name].at[r], m_["YR" + name].at[r], sem_y[name] + i, device(fy=True)).start()
+
+    def act_z(name, i):
+        r = rows_of(i)
+        q = pl.ds(i * s.span, s.span)
+        arrived(m_["YR" + name].at[r], sem_y[name] + i, device(fy=True))
+        both = m_["KY" + name][r, :] + m_["YR" + name][r, :].astype(f32)
+        m_["AS" + name][q, :] = both.astype(bf16)
+        go(m_["AS" + name].at[q], m_["AR" + name].at[q], sem_a[name] + i, device(1))
+
+    def act_last(name, i):
+        r = rows_of(MB + i)
+        q = pl.ds(i * s.span, s.span)
+        arrived(m_["YR" + name].at[r], sem_y[name] + MB + i, device(fy=True))
+        arrived(m_["AR" + name].at[q], sem_a[name] + i, device(1))
+        return (
+            m_["KY" + name][r, :]
+            + m_["YR" + name][r, :].astype(f32)
+            + m_["AR" + name][q, :].astype(f32)
+        )
+
+    def act_sent(name):
+        for i in range(4):
+            r = rows_of(i)
+            send(m_["CS" + name].at[r], m_["CR" + name].at[r], sem_c[name] + i, device(fc=True)).wait_send()
+            send(m_["YS" + name].at[r], m_["YR" + name].at[r], sem_y[name] + i, device(fy=True)).wait_send()
+
+    def loop(n, body):
+        lax.fori_loop(0, n, lambda i, carry: (body(i), carry)[1], 0)
+
+    def at_micro(m):
+        return pl.ds(mo(m * s.span, s.span), s.span)
+
+    def norm_phase():
+        extra = XG[0, s.rows : s.rows + EXTRA, :].astype(f32)
+        gain, shift = extra[0:1], extra[1:2]
+
+        def body(m):
+            xv = XG[m // MB, pl.ds(mo((m % MB) * s.span, s.span), s.span), :].astype(f32)
+            mu = jnp.sum(xv, 1, keepdims=True) * (1.0 / s.model)
+            var = jnp.sum(xv * xv, 1, keepdims=True) * (1.0 / s.model) - mu * mu
+            inv = lax.rsqrt(var + epsilon)
+            r = at_micro(m)
+            MU[r, :] = mu
+            IV[r, :] = inv
+            NB[r, :] = ((xv - mu) * inv * gain + shift).astype(bf16)
+
+        loop(s.micro, body)
+
+    def masks(m):
+        extra = XG[m // MB, s.rows : s.rows + EXTRA, 0 : s.span].astype(f32)
+        row_id = lax.broadcasted_iota(jnp.int32, extra.shape, 0)
+        first = 2 + SEQS * (m % MB)
+
+        def length(k):
+            return jnp.sum(jnp.where(row_id == first + k, extra, 0.0), 0, keepdims=True)
+
+        end0 = length(0)
+        end1 = end0 + length(1)
+        t = lax.broadcasted_iota(jnp.int32, (s.span, s.span), 0).astype(f32)
+        u = lax.broadcasted_iota(jnp.int32, (s.span, s.span), 1).astype(f32)
+        start = jnp.where(t >= end1, end1, jnp.where(t >= end0, end0, 0.0))
+        return jnp.logical_and(u <= t, u >= start), t, u, start
+
+    def head_rows():
+        lane = lax.broadcasted_iota(jnp.int32, (1, s.half), 1)
+        return [jnp.where(lane // HD == h, 1.0, 0.0).astype(bf16) for h in range(2)], [
+            jnp.where(lane == h * HD, 1.0, 0.0).astype(bf16) for h in range(2)
+        ]
+
+    HIGH = lax.Precision.HIGH
+    HIGHEST = lax.Precision.HIGHEST
+    hf = s.half
+
+    def table_phase():
+        wide = dot(dot(dct[...], omega[...], precision=HIGHEST), rep[...], precision=HIGHEST)
+        m_["A2"][...] = wide * (ones16[...].astype(f32) * (16.0 * HD ** (-0.25)))
+
+    def fwd_phase():
+        def body(m):
+            r = at_micro(m)
+            wq = jnp.concatenate([WQ[0], WQ[1], WQ[2]], 1)
+            bias = jnp.concatenate(
+                [small[1:2, pl.ds(mo(k * s.width + zl * hf, hf), hf)] for k in range(3)], 1
+            )
+            p = (dot(NB[r, :], wq) + bias).astype(bf16)
+            w, v = p[:, : 2 * hf], p[:, 2 * hf :]
+            m_["VB"][r, :] = v
+            mask, t, u, start = masks(m)
+            pos = t[:, :hf] - start[:, :hf]
+            hot = jnp.where(pos == u[:, :hf], 1.0, 0.0).astype(bf16)
+            cs = dot(jnp.concatenate([hot, hot, hot], 1), tab[...])
+            m_["CSB"][r, :] = cs
+            cc = jnp.concatenate([cs[:, :hf], cs[:, :hf]], 1)
+            ss = jnp.concatenate([cs[:, hf:], cs[:, hf:]], 1)
+            wf = w.astype(f32)
+            rot = wf * cc + dot(w, swap[...]) * ss
+            m_["ROTV"][r, :] = rot
+            score = dot(rot, m_["A2"][...], precision=HIGH)
+            norm2 = dot(wf * wf, ones16[...].astype(f32), precision=HIGH)
+            ph = jnp.exp(score - norm2) * small[2:3, 0 : 2 * hf]
+            m_["PHF"][r, :] = ph
+            pb = ph.astype(bf16)
+            m_["PHB"][r, :] = pb
+            hm, _ = head_rows()
+            acc = jnp.zeros((s.span, 2 * hf), f32)
+            for h in range(2):
+                sc = dot(pb[:, :hf] * hm[h], pb[:, hf:], NT)
+                sm = jnp.where(mask, sc, 0.0).astype(bf16)
+                m_["SB"][m, h] = sm
+                rhs = jnp.concatenate([v * hm[h], jnp.broadcast_to(hm[h], v.shape)], 1)
+                acc = acc + dot(sm, rhs)
+            m_["ND"][r, :] = acc
+            m_["AT"][r, :] = (acc[:, :hf] / acc[:, hf:]).astype(bf16)
+
+        loop(s.micro, body)
+
+    def bwd_phase():
+        m_["QBG"][...] = jnp.zeros_like(m_["QBG"])
+
+        def body(m):
+            r = at_micro(m)
+            mask = masks(m)[0]
+            hm, hot = head_rows()
+            ag = dot(G[r, :], WO[...], NT)
+            nd = m_["ND"][r, :]
+            num, den = nd[:, :hf], nd[:, hf:]
+            ng = (ag / den).astype(bf16)
+            sums = dot(ag * num, ones16[0:hf, 0:hf].astype(f32), precision=HIGH) * 16.0
+            dg = (-sums / (den * den)).astype(bf16)
+            v = m_["VB"][r, :]
+            pb = m_["PHB"][r, :]
+            v1 = jnp.concatenate([v, jnp.ones(v.shape, bf16)], 1)
+            dq = dk = dv = jnp.zeros((s.span, hf), f32)
+            for h in range(2):
+                e = dot(jnp.concatenate([ng * hm[h], dg * hot[h]], 1), v1, NT)
+                em = jnp.where(mask, e, 0.0).astype(bf16)
+                dq = dq + dot(em, pb[:, hf:] * hm[h])
+                dk = dk + dot(em, pb[:, :hf] * hm[h], TN)
+                dv = dv + dot(m_["SB"][m, h], ng * hm[h], TN)
+            dph = jnp.concatenate([dq, dk], 1) * m_["PHF"][r, :]
+            rot = m_["ROTV"][r, :]
+            both = dot(dph, ones16[...].astype(f32), precision=HIGH) * 2.0
+            drot = dot(dph, m_["A2"][...], NT, precision=HIGH) - rot * both
+            cs = m_["CSB"][r, :]
+            cc = jnp.concatenate([cs[:, :hf], cs[:, :hf]], 1)
+            ss = jnp.concatenate([cs[:, hf:], cs[:, hf:]], 1)
+            dw = drot * cc + dot(drot * ss, swap[...].astype(f32), NT, precision=HIGH)
+            pg = jnp.concatenate([dw, dv], 1).astype(bf16)
+            m_["PG"][r, :] = pg
+            m_["QBG"][...] += jnp.sum(pg.astype(f32), 0, keepdims=True)
+
+        loop(s.micro, body)
+
+    def up_phase():
+        bias = small[0:1, lanes(zl, s.hidden)]
+
+        def body(m):
+            r = at_micro(m)
+            pre = dot(NB[r, :], WU[...]) + bias
+            cdf = 0.5 * (1.0 + lax.erf(pre * math.sqrt(0.5)))
+            m_["HB"][r, :] = (pre * cdf).astype(bf16)
+            m_["GP"][r, :] = cdf + pre * jnp.exp(-0.5 * pre * pre) * (1.0 / math.sqrt(2.0 * math.pi))
+
+        loop(s.micro, body)
+
+    def pre_phase():
+        m_["UBG"][...] = jnp.zeros_like(m_["UBG"])
+
+        def body(m):
+            r = at_micro(m)
+            pre = (dot(G[r, :], WD[...], NT) * m_["GP"][r, :]).astype(bf16)
+            m_["PRE"][r, :] = pre
+            m_["UBG"][...] += jnp.sum(pre.astype(f32), 0, keepdims=True)
+
+        loop(s.micro, body)
+
+    def nrm_phase():
+        def body(i):
+            r = rows_of(i)
+            wq = jnp.concatenate([WQ[0], WQ[1], WQ[2]], 1)
+            act_put("nrm", i, dot(m_["PG"][r, :], wq, NT) + dot(m_["PRE"][r, :], WU[...], NT))
+
+        loop(4, body)
+
+    def blk_phase():
+        def body(i):
+            r = rows_of(i)
+            act_put("blk", i, dot(m_["AT"][r, :], WO[...]) + dot(m_["HB"][r, :], WD[...]))
+
+        loop(4, body)
+
+    two = 2 * s.block
+
+    def grad_phase(w):
+        def body(zp):
+            cols = lanes(zp, two)
+            if w == "qkv":
+                value = dot(NB[:, cols], m_["PG"][...], TN)
+                mine, theirs = halves(value, 0)
+                mine = jnp.stack([mine[:, k * hf : (k + 1) * hf] for k in range(3)], 0)
+                theirs = jnp.stack([theirs[:, k * hf : (k + 1) * hf] for k in range(3)], 0)
+            elif w == "up":
+                mine, theirs = halves(dot(NB[:, cols], m_["PRE"][...], TN), 0)
+            elif w == "out":
+                mine, theirs = halves(dot(m_["AT"][...], G[:, cols], TN), 1)
+            else:
+                mine, theirs = halves(dot(m_["HB"][...], G[:, cols], TN), 1)
+            put_grad(w, zp, mine, theirs)
+
+        loop(s.planes, body)
+
+    def out_rows(i):
+        return pl.ds(i * s.span, s.span)
+
+    def blk_last():
+        for i in range(MB):
+            own = XG[zl, i * s.span : (i + 1) * s.span, lanes(ft, s.width)].astype(f32)
+            bias = small[1:2, 3 * s.width : 4 * s.width]
+            o_blk[out_rows(i), :] = (own + act_last("blk", i) + bias).astype(bf16)
+
+    sem_st = new(3)
+    stat_where = [device(fc=True), device(fy=True), device(fy=True, fc=True)]
+
+    def own_parts():
+        extra = XG[0, s.rows : s.rows + EXTRA, lanes(ft, s.width)].astype(f32)
+        r = lanes(zl, s.rows)
+        own = XG[zl, 0 : s.rows, lanes(ft, s.width)].astype(f32)
+        xhat = (own - MU[r, :]) * IV[r, :]
+        return extra[0:1], xhat
+
+    def nrm_last():
+        for i in range(MB):
+            m_["NGF"][out_rows(i), :] = act_last("nrm", i)
+        gain, xhat = own_parts()
+        ngrad = m_["NGF"][...]
+        scaled = ngrad * gain
+        ones = jnp.ones((8, s.width), f32)
+        m_["ST"][0:8, :] = dot(ones, scaled, NT, precision=HIGHEST)
+        m_["ST"][8:16, :] = dot(ones, scaled * xhat, NT, precision=HIGHEST)
+        for k, where in enumerate(stat_where):
+            go(m_["ST"], m_["STR"].at[k], sem_st + k, where)
+        own_g = G[lanes(zl, s.rows), lanes(ft, s.width)].astype(f32)
+        rows = [
+            jnp.sum(ngrad * xhat, 0, keepdims=True),
+            jnp.sum(ngrad, 0, keepdims=True),
+            jnp.sum(own_g, 0, keepdims=True),
+        ]
+        sv = m_["SV"]
+        sv[...] = jnp.zeros_like(sv)
+        for k, row in enumerate(rows):
+            for j in range(2):
+                sv[2 * k + j : 2 * k + j + 1, :] = row[:, j * 128 : (j + 1) * 128]
+        for k in range(3):
+            sv[pl.ds(6 + 2 * k + zl, 1), :] = m_["QBG"][0:1, k * hf : (k + 1) * hf]
+        for j in range(s.hidden // 128):
+            sv[pl.ds(12 + zl * (s.hidden // 128) + j, 1), :] = m_["UBG"][0:1, j * 128 : (j + 1) * 128]
+
+    sem_sv = new(7)
+    sv_where = [device(d) for d in (1, 2, 3)] + [device(d, fx=True) for d in (0, 1, 2, 3)]
+
+    def small_send():
+        for k, where in enumerate(sv_where):
+            go(m_["SV"], m_["SVR"].at[k], sem_sv + k, where)
+
+    def small_last():
+        total = m_["SV"][...]
+        for k, where in enumerate(sv_where):
+            arrived(m_["SVR"].at[k], sem_sv + k, where)
+            total = total + m_["SVR"][k]
+        o_small[...] = total
+
+    def input_last():
+        total = m_["ST"][...]
+        for k, where in enumerate(stat_where):
+            arrived(m_["STR"].at[k], sem_st + k, where)
+            total = total + m_["STR"][k]
+        spread = jnp.full((8, s.width), 1.0 / (8.0 * s.model), f32)
+        mean1 = dot(total[0:8, :], spread, TN, precision=HIGHEST)
+        mean2 = dot(total[8:16, :], spread, TN, precision=HIGHEST)
+        gain, xhat = own_parts()
+        own_g = G[lanes(zl, s.rows), lanes(ft, s.width)].astype(f32)
+        scaled = m_["NGF"][...] * gain
+        inv = IV[lanes(zl, s.rows), :]
+        o_inp[...] = (own_g + inv * (scaled - mean1 - xhat * mean2)).astype(bf16)
+
+    act_first("tok", tok_at)
+    w_own("qkv")
+    w_z("qkv")
+    w_own("out")
+    table_phase()
+    act_forward("tok", tok_at)
+    act_first("grd", grd_at)
+    w_z("out")
+    w_z("up")
+    w_z("down")
+    for d in (1, 2, 3):
+        w_forward("qkv", d)
+    w_own("up")
+    w_own("down")
+    act_rest("tok", tok_at)
+    norm_phase()
+    act_forward("grd", grd_at)
+    for d in (1, 2, 3):
+        w_forward("out", d)
+    w_rest("qkv")
+    fwd_phase()
+    act_rest("grd", grd_at)
+    for d in (1, 2, 3):
+        w_forward("up", d)
+    w_rest("out")
+    bwd_phase()
+    grad_phase("out")
+    grad_phase("qkv")
+    for d in (1, 2, 3):
+        w_forward("down", d)
+    w_rest("up")
+    up_phase()
+    grad_z("out")
+    grad_z("qkv")
+    w_rest("down")
+    pre_phase()
+    nrm_phase()
+    blk_phase()
+    for i in range(4):
+        act_y("nrm", i)
+    grad_phase("up")
+    for i in range(4):
+        act_y("blk", i)
+    for i in range(2):
+        act_z("nrm", i)
+    grad_phase("down")
+    for i in range(2):
+        act_z("blk", i)
+    grad_z("up")
+    nrm_last()
+    small_send()
+    grad_z("down")
+    blk_last()
+    input_last()
+    small_last()
+    for w in ws:
+        grad_last(w)
+    for copy in sent:
+        copy.wait_send()
+    for name in ("blk", "nrm"):
+        act_sent(name)
+    assert counter[0] <= N_REMOTE
+
+
+def on_device_fused(
+    dp_count,
+    feat_count,
+    tokens,
+    doc_lengths,
+    norm_gain,
+    norm_shift,
+    qkv_weight,
+    qkv_bias,
+    omega,
+    qmc_weights,
+    out_weight,
+    out_bias,
+    up_weight,
+    up_bias,
+    down_weight,
+    out_grad,
+):
+    rows, width = tokens.shape
+    s = Sizes(rows, width, up_weight.shape[1], dp_count, feat_count)
+    lens = jnp.broadcast_to(doc_lengths.reshape(-1, 1).astype(bf16), (doc_lengths.size, width))
+    extra = jnp.concatenate(
+        [
+            norm_gain[None],
+            norm_shift[None],
+            lens,
+            jnp.zeros((EXTRA - 2 - doc_lengths.size, width), bf16),
+        ],
+        0,
+    )
+    full = up_bias.shape[0]
+    lane_gain = jnp.concatenate([qmc_weights, qmc_weights, jnp.ones((width // 2,), f32)])
+    small = jnp.stack(
+        [
+            up_bias.astype(f32),
+            jnp.concatenate([qkv_bias.reshape(-1), out_bias]).astype(f32),
+            jnp.concatenate([lane_gain, jnp.zeros((full - lane_gain.shape[0],), f32)]),
+        ],
+        0,
+    )
+    ones16 = np.kron(np.eye(4), np.full((HD, HD), 1.0 / 16.0)).astype(ml_dtypes.bfloat16)
+    rep = np.tile(np.eye(HD, dtype=np.float32), (1, 4))
+    shapes = scratch_list(s)
+    names = list(shapes) + ["lsem", "ssem", "rsem"]
+    scratch = [pltpu.VMEM(shape, kind) for shape, kind in shapes.values()]
+    scratch += [
+        pltpu.SemaphoreType.DMA((N_LOCAL,)),
+        pltpu.SemaphoreType.DMA((N_REMOTE,)),
+        pltpu.SemaphoreType.DMA((N_REMOTE,)),
+    ]
+    raw = pl.BlockSpec(memory_space=pl.ANY)
+    vm = pl.BlockSpec(memory_space=pltpu.VMEM)
+    outs = pl.pallas_call(
+        functools.partial(fused_kernel, s, names),
+        out_shape=(
+            jax.ShapeDtypeStruct((rows, width), bf16),
+            jax.ShapeDtypeStruct((rows, width), bf16),
+            jax.ShapeDtypeStruct((3, s.block, width), f32),
+            jax.ShapeDtypeStruct(up_weight.shape, f32),
+            jax.ShapeDtypeStruct(out_weight.shape, f32),
+            jax.ShapeDtypeStruct(down_weight.shape, f32),
+            jax.ShapeDtypeStruct((24, 128), f32),
+        ),
+        in_specs=[raw] * 7 + [vm] * 7,
+        out_specs=[vm] * 7,
+        scratch_shapes=scratch,
+        compiler_params=pltpu.CompilerParams(
+            collective_id=0, has_side_effects=True, vmem_limit_bytes=63 * 2**20
+        ),
+    )(
+        tokens,
+        out_grad,
+        extra,
+        jnp.transpose(qkv_weight, (1, 0, 2)),
+        up_weight,
+        out_weight,
+        down_weight,
+        small,
+        jnp.asarray(rotary_table(rows // MB // 2)),
+        jnp.asarray(rotary_swap()),
+        jnp.asarray(ones16),
+        jnp.asarray(dct_rows()),
+        jnp.asarray(rep),
+        omega,
+    )
+    o_blk, o_inp, o_qkv, o_up, o_out, o_down, o_small = outs
+    flat = o_small.reshape(-1)
+    return (
+        o_blk,
+        o_inp,
+        flat[0:width],
+        flat[width : 2 * width],
+        jnp.transpose(o_qkv, (1, 0, 2)),
+        flat[3 * width : 6 * width].reshape(3, width),
+        o_out,
+        flat[2 * width : 3 * width],
+        o_up,
+        flat[6 * width : 6 * width + full],
+        o_down,
+    )
+
+
 def solution(mesh):
     in_specs = (
         P("dp", "feat"),
@@ -419,6 +1224,11 @@
         P("feat"),
         P("feat", "dp"),
     )
+    dp_count, feat_count = mesh.shape["dp"], mesh.shape["feat"]
+    if (dp_count, feat_count) == (8, 4):
+        per_device = functools.partial(on_device_fused, dp_count, feat_count)
+    else:
+        per_device = on_device
     return jax.shard_map(
-        on_device, mesh=mesh, in_specs=in_specs, out_specs=out_specs, check_vma=False
-    )
+        per_device, mesh=mesh, in_specs=in_specs, out_specs=out_specs, check_vma=False
+    )

time: 966 us -> 137 us (0.14); the launches traced: 947 us -> 137 us
  waiting for transfers between devices: 391 us -> 0 us
  local copies, waits for them, and re-layouts: 215 us -> 12.7 us
  matrix products: 140 us -> 0 us
  blocking collectives: 130 us -> 0 us
  Pallas kernels: 0 us -> 122 us
  other arithmetic: 50.4 us -> 1.38 us
  between operations: 18.7 us -> 0.7 us
    reduce_scatter x10 -> x0, waiting for transfers between devices: 182 us -> none  [the longest x1 69 us: on_device(): lax.psum_scatter(up_acc.astype(jnp.bfloat16), 'dp', scatter_dimension=0,...]
    dot_general x64 -> x0, matrix products: 140 us -> none  [the longest x8 15.7 us: feature_map(): spectrum = jnp.einsum('rhn,kn->rhk', turned, dct_table(), precision=highest)]
    unnamed x20 -> x0, waiting for transfers between devices: 124 us -> none
    pallas_call x0 -> x1, Pallas kernels: none -> 122 us  [on_device_fused(): pl.pallas_call(functools.partial(fused_kernel, s, names), out_shape=(jax....]
    all_gather x6 -> x0, waiting for transfers between devices: 85.1 us -> none  [the longest x1 46.4 us: on_device(): lax.all_gather(qkv_weight, 'dp', axis=0, tiled=True)]
    unnamed x293 -> x33, local copies, waits for them, and re-layouts: 84.1 us -> 10.7 us
    all_gather x7 -> x0, blocking collectives: 66.6 us -> none  [the longest x1 27.3 us: on_device(): lax.all_gather(out_weight, 'dp', axis=1, tiled=True)]
    psum x3 -> x0, blocking collectives: 51.4 us -> none  [the longest x1 37.3 us: on_device(): lax.psum((gain_part, shift_part, qkv_bias_acc, out_bias_part, up_bias_acc...]
  transfers between devices with their start and end apart: 18 -> 0, of which waited for: 12 -> 0; matrix products, arithmetic and copies ran while one was open for 32% -> 0% of each run, Pallas kernels for 0% -> 0%
where the time goes in v1:
time: 137 us
  Pallas kernels  122 us (89%)
  local copies, waits for them, and re-layouts  12.7 us (9%)
  other arithmetic  1.38 us (1%)
    pallas_call x1, Pallas kernels, on_device_fused(): pl.pallas_call(functools.partial(fused_kernel, s, names), out_shape=(jax....  122 us
    unnamed x33, local copies, waits for them, and re-layouts  10.7 us

profile of v1, /device:TPU:0, one launch (start us, length us, event | category | flops | bytes accessed | tf_op | source)
XLA Modules:
  0.0 136.9 jit_solution(4771649721783119145)
XLA Ops:
  0.6 0.0 copy-start.9
  0.7 0.7 copy-done.9
  1.3 0.1 reshape.74
  1.4 0.1 pad.11.clone
  1.5 0.0 copy-start.10
  1.5 0.1 pad.12.clone
  1.6 0.6 copy-done.10
  2.2 0.0 copy-start.11
  2.2 0.0 copy-start.12
  2.2 0.6 copy-done.11
  2.8 0.0 copy-start.7
  2.8 0.0 copy-done.12
  2.8 0.7 copy-done.7
  3.5 0.0 copy-start.6
  3.5 0.7 copy-done.6
  4.2 0.0 copy-start.8
  4.2 0.6 copy-done.8
  4.8 0.1 pad_maximum_fusion.1
  4.9 0.6 pad_maximum_fusion.refs_7_
  5.5 0.7 maximum_maximum_fusion.refs_2_
  6.2 122.1 %shard_map.266 = (bf16[512,256]{1,0:T(8,128)(2,1)}, bf16[512,256]{1,0:T(8,128)(2,1)}, f32[3,128,256]{2,1,0:T(8,128)}, f32[128,1024]{1,0:T(8,128)}, f32[256,128]{...) custom-call(bf16[512,256]{1,0:T(8,128)(2,1)} %refs_0_.1, bf16[512,256]{1,0:T(8,128)(2,1)} %refs_1_.1, ...), custom_call_target="tpu_custom_call" | custom-call | tf_op jit(solution)/shard_map/pallas_call | solution.py:1147
  128.3 0.0 copy-start.5
  128.3 0.7 copy-done.5
  129.0 0.6 slice_bitcast_fusion.1
  129.6 0.6 slice_bitcast_fusion
  130.2 0.0 copy-start.3
  130.2 0.6 reshape.72
  130.8 0.0 copy-start.2
  130.8 1.7 %copy.37 = bf16[512,256]{1,0:T(8,128)(2,1)} copy(bf16[512,256]{1,0:T(8,128)(2,1)} %get-tuple-element.39) | data formatting | bytes 524288
  132.5 0.0 copy-done.3
  132.5 0.7 copy.38
  133.2 0.0 copy-done.2
  133.2 0.0 copy-start.4
  133.2 0.0 copy-start.1
  133.2 0.7 copy.39
  134.0 0.2 copy-done.4
  134.2 0.7 copy.40
  134.9 0.0 copy-done.1
  134.9 0.0 copy-start
  134.9 0.8 copy.41
  135.7 0.4 copy-done
  136.1 0.8 copy.42
  (11 shorter events, 0.0 us)
Async XLA Ops:
  0.6 0.7 copy-start.9
  1.5 0.7 copy-start.10
  2.2 0.7 copy-start.11
  2.2 0.7 copy-start.12
  2.8 0.7 copy-start.7
  3.5 0.7 copy-start.6
  4.2 0.7 copy-start.8
  128.3 0.7 copy-start.5
  130.2 2.3 %copy-start.3 = (bf16[512,256]{1,0:T(8,128)(2,1)S(1)}, bf16[512,256]{1,0:T(8,128)(2,1)}, u32[]{:S(2)}) copy-start(bf16[512,256]{1,0:T(8,128)(2,1)} %get-tuple-element.40) | copy-start | bytes 786436
  130.8 2.4 %copy-start.2 = (f32[3,128,256]{2,1,0:T(8,128)S(1)}, f32[3,128,256]{2,1,0:T(8,128)}, u32[]{:S(2)}) copy-start(f32[3,128,256]{2,1,0:T(8,128)} %get-tuple-element.21) | copy-start | bytes 1179652
  133.2 1.0 copy-start.4
  133.2 1.7 %copy-start.1 = (f32[128,1024]{1,0:T(8,128)S(1)}, f32[128,1024]{1,0:T(8,128)}, u32[]{:S(2)}) copy-start(f32[128,1024]{1,0:T(8,128)} %get-tuple-element.47) | copy-start | bytes 1572868
  134.9 1.2 copy-start

commit v2 on v1

--- a/solution.py
+++ b/solution.py
@@ -17,6 +17,18 @@
 SPAN = 64
 MB = 2
 SEQS = 3
+
+
+FEAT = "feat"
+DP = "dp"
+QKV = "qkv"
+OUT = "out"
+UP = "up"
+DOWN = "down"
+TOK = "tok"
+GRD = "grd"
+NRM = "nrm"
+BLK = "blk"
 
 
 epsilon = 1e-05
@@ -180,24 +192,24 @@
     down_weight,
     out_grad,
 ):
-    feat_parts = lax.axis_size("feat")
-    feat_index = lax.axis_index("feat")
+    feat_parts = lax.axis_size(FEAT)
+    feat_index = lax.axis_index(FEAT)
     qkv_full, up_full, out_rows, down_rows = (
-        lax.all_gather(qkv_weight, "dp", axis=0, tiled=True),
-        lax.all_gather(up_weight, "dp", axis=0, tiled=True),
-        lax.all_gather(out_weight, "dp", axis=1, tiled=True),
-        lax.all_gather(down_weight, "dp", axis=1, tiled=True),
+        lax.all_gather(qkv_weight, DP, axis=0, tiled=True),
+        lax.all_gather(up_weight, DP, axis=0, tiled=True),
+        lax.all_gather(out_weight, DP, axis=1, tiled=True),
+        lax.all_gather(down_weight, DP, axis=1, tiled=True),
     )
     gain_vec = norm_gain.astype(jnp.float32)
     shift_vec = norm_shift.astype(jnp.float32)
     inputs = tokens.astype(jnp.float32)
-    row_sums = lax.psum((jnp.sum(inputs, 1), jnp.sum(inputs * inputs, 1)), "feat")
+    row_sums = lax.psum((jnp.sum(inputs, 1), jnp.sum(inputs * inputs, 1)), FEAT)
     center = row_sums[0] / D
     spread = row_sums[1] / D - center * center
     inv_root = lax.rsqrt(spread + epsilon)
     standard = (inputs - center[:, None]) * inv_root[:, None]
     normed_all = lax.all_gather(
-        (standard * gain_vec + shift_vec).astype(jnp.bfloat16), "feat", axis=1, tiled=True
+        (standard * gain_vec + shift_vec).astype(jnp.bfloat16), FEAT, axis=1, tiled=True
     )
     local_width = tokens.shape[1]
     local_heads = local_width // HD
@@ -221,7 +233,7 @@
         ).astype(jnp.bfloat16)
         pre_act = jnp.dot(normed_rows, up_full, preferred_element_type=jnp.float32) + up_bias_f
         hidden = gelu_exact(pre_act).astype(jnp.bfloat16)
-        projected_used = lax.all_gather(projected, "feat", axis=2, tiled=True)
+        projected_used = lax.all_gather(projected, FEAT, axis=2, tiled=True)
         heads_used = projected_used.shape[2] // HD
         heads_view = projected_used.astype(jnp.float32).reshape(row_count, 3, heads_used, HD)
         queries = heads_view[:, 0]
@@ -236,8 +248,8 @@
         numerator = mixed[..., :HD]
         denominator = mixed[..., HD]
         numerator, denominator = (
-            lax.psum_scatter(numerator, "feat", scatter_dimension=1, tiled=True),
-            lax.psum_scatter(denominator, "feat", scatter_dimension=1, tiled=True),
+            lax.psum_scatter(numerator, FEAT, scatter_dimension=1, tiled=True),
+            lax.psum_scatter(denominator, FEAT, scatter_dimension=1, tiled=True),
         )
         attended = (
             (numerator / denominator[..., None])
@@ -247,7 +259,7 @@
         branch = jnp.dot(attended, out_rows, preferred_element_type=jnp.float32)
         branch = branch + jnp.dot(hidden, down_rows, preferred_element_type=jnp.float32)
         summed = lax.psum_scatter(
-            branch.astype(jnp.bfloat16), "feat", scatter_dimension=1, tiled=True
+            branch.astype(jnp.bfloat16), FEAT, scatter_dimension=1, tiled=True
         ).astype(jnp.float32)
         block_outs.append(
             (inputs[offset : offset + row_count] + summed + out_bias_f).astype(jnp.bfloat16)
@@ -294,7 +306,7 @@
             attended,
         ) = saved_state[micro_idx]
         cotangent = lax.all_gather(
-            out_grad[offset : offset + row_count], "feat", axis=1, tiled=True
+            out_grad[offset : offset + row_count], FEAT, axis=1, tiled=True
         )
         outw_acc = outw_acc + jnp.einsum(
             "rk,rd->kd", attended, cotangent, preferred_element_type=jnp.float32
@@ -318,8 +330,8 @@
             jnp.bfloat16
         )
         numer_grad, denom_grad = (
-            lax.all_gather(numer_grad, "feat", axis=1, tiled=True),
-            lax.all_gather(denom_grad, "feat", axis=1, tiled=True),
+            lax.all_gather(numer_grad, FEAT, axis=1, tiled=True),
+            lax.all_gather(denom_grad, FEAT, axis=1, tiled=True),
         )
         upstream = jnp.concatenate(
             [numer_grad.astype(jnp.float32), denom_grad.astype(jnp.float32)[..., None]], 2
@@ -336,7 +348,7 @@
         proj_rows = jnp.stack([query_grad, key_grad, extended_grad[..., :HD]], 1).reshape(
             row_count, 3, -1
         )
-        proj_rows = lax.psum_scatter(proj_rows, "feat", scatter_dimension=2, tiled=True)
+        proj_rows = lax.psum_scatter(proj_rows, FEAT, scatter_dimension=2, tiled=True)
         proj_grad = proj_rows.astype(jnp.bfloat16)
         qkv_acc = qkv_acc + jnp.einsum(
             "rd,rcf->dcf", normed_rows, proj_grad, preferred_element_type=jnp.float32
@@ -350,12 +362,12 @@
         )
         normed_grads.append(
             lax.psum_scatter(
-                normed_part.astype(jnp.bfloat16), "feat", scatter_dimension=1, tiled=True
+                normed_part.astype(jnp.bfloat16), FEAT, scatter_dimension=1, tiled=True
             ).astype(jnp.float32)
         )
     normed_grad = jnp.concatenate(normed_grads, 0)
     scaled = normed_grad * gain_vec
-    grad_sums = lax.psum((jnp.sum(scaled, 1), jnp.sum(scaled * standard, 1)), "feat")
+    grad_sums = lax.psum((jnp.sum(scaled, 1), jnp.sum(scaled * standard, 1)), FEAT)
     out_grad_f = out_grad.astype(jnp.float32)
     input_grad = out_grad_f + inv_root[:, None] * (
         scaled - grad_sums[0][:, None] / D - standard * grad_sums[1][:, None] / D
@@ -365,20 +377,20 @@
     out_bias_part = jnp.sum(out_grad_f, 0)
     qkv_grad, up_grad, outw_grad, down_grad = (
         lax.psum_scatter(
-            qkv_acc.astype(jnp.bfloat16), "dp", scatter_dimension=0, tiled=True
+            qkv_acc.astype(jnp.bfloat16), DP, scatter_dimension=0, tiled=True
         ).astype(jnp.float32),
-        lax.psum_scatter(up_acc.astype(jnp.bfloat16), "dp", scatter_dimension=0, tiled=True).astype(
+        lax.psum_scatter(up_acc.astype(jnp.bfloat16), DP, scatter_dimension=0, tiled=True).astype(
             jnp.float32
         ),
         lax.psum_scatter(
-            outw_acc.astype(jnp.bfloat16), "dp", scatter_dimension=1, tiled=True
+            outw_acc.astype(jnp.bfloat16), DP, scatter_dimension=1, tiled=True
         ).astype(jnp.float32),
         lax.psum_scatter(
-            down_acc.astype(jnp.bfloat16), "dp", scatter_dimension=1, tiled=True
+            down_acc.astype(jnp.bfloat16), DP, scatter_dimension=1, tiled=True
         ).astype(jnp.float32),
     )
     gain_grad, shift_grad, qkv_bias_grad, out_bias_grad, up_bias_grad = lax.psum(
-        (gain_part, shift_part, qkv_bias_acc, out_bias_part, up_bias_acc), "dp"
+        (gain_part, shift_part, qkv_bias_acc, out_bias_part, up_bias_acc), DP
     )
     return (
         jnp.concatenate(block_outs, 0),
@@ -463,10 +475,10 @@
 def scratch_list(s):
     pl_, bl, hf, hd, tt, md = s.planes, s.block, s.half, s.hidden, s.total, s.model
     grads = {
-        "qkv": (3, bl, hf),
-        "out": (hf, bl),
-        "up": (bl, hd),
-        "down": (hd, bl),
+        QKV: (3, bl, hf),
+        OUT: (hf, bl),
+        UP: (bl, hd),
+        DOWN: (hd, bl),
     }
     shapes = dict(
         XG=((2, s.rows + EXTRA, md), bf16),
@@ -498,6 +510,20 @@
         ST=((16, s.rows), f32),
         STR=((3, 16, s.rows), f32),
         SV=((24, 128), f32),
+        SMALL=((3, max(2 * hd, 4 * s.width)), f32),
+        IN_lens=((MB, SEQS), jnp.int32),
+        IN_gain=((s.width,), bf16),
+        IN_shift=((s.width,), bf16),
+        IN_qkv_bias=((3, s.width), bf16),
+        IN_out_bias=((s.width,), bf16),
+        IN_up_bias=((2 * hd,), bf16),
+        IN_qmc=((M,), f32),
+        IN_tab=((3 * (s.span // 2), 2 * hf), bf16),
+        IN_swap=((2 * hf, 2 * hf), bf16),
+        IN_ones16=((2 * hf, 2 * hf), bf16),
+        IN_dct=((2 * hf, HD), f32),
+        IN_rep=((HD, 2 * hf), f32),
+        IN_omega=((HD, M), f32),
         SVR=((7, 24, 128), f32),
     )
     for name, shape in grads.items():
@@ -506,7 +532,7 @@
         shapes["KX" + name] = ((pl_,) + shape, f32)
         shapes["ZS" + name] = ((3,) + shape, bf16)
         shapes["ZR" + name] = ((3,) + shape, bf16)
-    for name in ("blk", "nrm"):
+    for name in (BLK, NRM):
         shapes["CS" + name] = ((tt, 2 * s.width), bf16)
         shapes["CR" + name] = ((tt, 2 * s.width), bf16)
         shapes["KC" + name] = ((tt, 2 * s.width), f32)
@@ -518,26 +544,35 @@
     return shapes
 
 
-N_LOCAL = 7
+SMALL = ("lens", "gain", "shift", "qkv_bias", "out_bias", "up_bias", "qmc", "tab", "swap", "ones16", "dct", "rep", "omega")
+N_LOCAL = 6 + len(SMALL)
 N_REMOTE = 120
 
 
 def fused_kernel(s, names, *refs):
-    (tok, grd, ext, wq_in, wu_in, wo_in, wd_in, small, tab, swap, ones16, dct, rep, omega) = refs[:14]
-    o_blk, o_inp, o_qkv, o_up, o_out, o_down, o_small = refs[14:21]
-    m_ = dict(zip(names, refs[21:]))
+    (tok, grd, wq_in, wu_in, wo_in, wd_in) = refs[:6]
+    small_in = refs[6 : 6 + len(SMALL)]
+    o_blk, o_inp, o_qkv, o_up, o_out, o_down, o_small = refs[6 + len(SMALL) : 13 + len(SMALL)]
+    m_ = dict(zip(names, refs[13 + len(SMALL) :]))
+    small, tab, swap, ones16 = m_["SMALL"], m_["IN_tab"], m_["IN_swap"], m_["IN_ones16"]
+    dct, rep, omega = m_["IN_dct"], m_["IN_rep"], m_["IN_omega"]
     lsem, ssem, rsem = m_["lsem"], m_["ssem"], m_["rsem"]
     XG, G, WQ, WU, WO, WD = (m_[k] for k in ("XG", "G", "WQ", "WU", "WO", "WD"))
     NB, MU, IV = m_["NB"], m_["MU"], m_["IV"]
 
-    dp = lax.axis_index("dp")
-    ft = lax.axis_index("feat")
+    dp = lax.axis_index(DP)
+    ft = lax.axis_index(FEAT)
     z, x = dp // 2, dp % 2
     zl = z % 2
     y, c = ft // 2, ft % 2
-    zd = (z, z + 1 - 2 * zl, z + 2 - 4 * (z // 2), 3 - z)
-    zd = (z, z + 1 - 2 * zl, (z + 2) % 4, z + 1 - 2 * zl + 2 - 4 * (z // 2))
+    zd = (z, z + 1 - 2 * zl, (z + 2) % 4, 3 - z)
     hl = (zl, 1 - zl, zl, 1 - zl)
+
+    def partner(d):
+        if isinstance(d, int):
+            return zd[d]
+        return (z // 2 + d // 2) % 2 * 2 + (z + d) % 2
+
     counter = [0]
 
     def new(n=1):
@@ -546,8 +581,8 @@
 
     def device(d=0, fx=False, fy=False, fc=False):
         return {
-            "dp": zd[d] * 2 + (1 - x if fx else x),
-            "feat": (1 - y if fy else y) * 2 + (1 - c if fc else c),
+            DP: partner(d) * 2 + (1 - x if fx else x),
+            FEAT: (1 - y if fy else y) * 2 + (1 - c if fc else c),
         }
 
     def send(src, dst, sem, where):
@@ -561,12 +596,8 @@
         )
         return copy
 
-    sent = []
-
     def go(src, dst, sem, where):
-        copy = send(src, dst, sem, where)
-        copy.start()
-        sent.append(copy)
+        send(src, dst, sem, where).start()
 
     def arrived(ref, sem, where):
         send(ref, ref, sem, where).wait_recv()
@@ -583,32 +614,33 @@
         return G.at[lanes(b, s.rows), lanes(f, s.width)]
 
     def own_half(w, h):
-        if w == "qkv":
+        if w == QKV:
             return wq_in.at[:, :, lanes(h, s.half)]
-        if w == "up":
+        if w == UP:
             return wu_in.at[:, lanes(h, s.hidden)]
-        if w == "out":
+        if w == OUT:
             return wo_in.at[lanes(h, s.half), :]
         return wd_in.at[lanes(h, s.hidden), :]
 
     def weight_at(w, block):
-        if w == "qkv":
+        if w == QKV:
             return WQ.at[:, lanes(block, s.block), :]
-        if w == "up":
+        if w == UP:
             return WU.at[lanes(block, s.block), :]
-        if w == "out":
+        if w == OUT:
             return WO.at[:, lanes(block, s.block)]
         return WD.at[:, lanes(block, s.block)]
 
-    ws = ("qkv", "out", "up", "down")
+    ws = (QKV, OUT, UP, DOWN)
 
     local = [
         pltpu.make_async_copy(tok, XG.at[zl, pl.ds(0, s.rows), lanes(ft, s.width)], lsem.at[0]),
-        pltpu.make_async_copy(ext, XG.at[zl, pl.ds(s.rows, EXTRA), lanes(ft, s.width)], lsem.at[1]),
-        pltpu.make_async_copy(grd, grd_at(zl, ft), lsem.at[2]),
+        pltpu.make_async_copy(grd, grd_at(zl, ft), lsem.at[1]),
     ]
     for i, w in enumerate(ws):
-        local.append(pltpu.make_async_copy(own_half(w, zl), weight_at(w, dp), lsem.at[3 + i]))
+        local.append(pltpu.make_async_copy(own_half(w, zl), weight_at(w, dp), lsem.at[2 + i]))
+    for i, name in enumerate(SMALL):
+        local.append(pltpu.make_async_copy(small_in[i], m_["IN_" + name], lsem.at[6 + i]))
     for copy in local:
         copy.start()
 
@@ -621,25 +653,44 @@
     for copy in local:
         copy.wait()
 
-    sem_act = {"tok": new(7), "grd": new(7)}
-
-    def act_first(name, at):
-        base = sem_act[name]
-        go(at(zl, ft), at(zl, ft), base + 1, device(fy=True))
-        go(at(zl, ft), at(zl, ft), base + 2, device(1))
-        go(at(zl, ft), at(zl, ft), base + 0, device(fc=True))
-
-    def act_forward(name, at):
+    def row_of(name):
+        value = m_["IN_" + name][...].astype(f32)
+        return value.reshape(1, value.shape[0])
+
+    lens = m_["IN_lens"][...].astype(f32)
+    rows = [row_of("gain"), row_of("shift")]
+    for i in range(MB):
+        for j in range(SEQS):
+            rows.append(jnp.broadcast_to(lens[i : i + 1, j : j + 1], (1, s.width)))
+    rows.append(jnp.zeros((EXTRA - len(rows), s.width), f32))
+    XG[zl, s.rows : s.rows + EXTRA, lanes(ft, s.width)] = jnp.concatenate(rows, 0).astype(bf16)
+    small[0:1, 0 : 2 * s.hidden] = row_of("up_bias")
+    for k in range(3):
+        small[1:2, k * s.width : (k + 1) * s.width] = m_["IN_qkv_bias"][k : k + 1, :].astype(f32)
+    small[1:2, 3 * s.width : 4 * s.width] = row_of("out_bias")
+    qmc = row_of("qmc")
+    small[2:3, 0 : 2 * s.half] = jnp.concatenate([qmc, qmc, jnp.ones((1, s.half), f32)], 1)
+
+    sem_act = {TOK: new(7), GRD: new(7)}
+
+    def act_own(name, at, axis):
+        k, where = {"c": (0, device(fc=True)), "y": (1, device(fy=True)), "z": (2, device(1))}[axis]
+        go(at(zl, ft), at(zl, ft), sem_act[name] + k, where)
+
+    def act_arrive(name, at, k):
         base = sem_act[name]
         fy = (1 - y) * 2 + c
         zb = 1 - zl
-        arrived(at(zb, ft), base + 2, device(1))
-        go(at(zb, ft), at(zb, ft), base + 3, device(fy=True))
-        go(at(zb, ft), at(zb, ft), base + 4, device(fc=True))
-        arrived(at(zl, fy), base + 1, device(fy=True))
-        go(at(zl, fy), at(zl, fy), base + 5, device(fc=True))
-        arrived(at(zb, fy), base + 3, device(fy=True))
-        go(at(zb, fy), at(zb, fy), base + 6, device(fc=True))
+        if k == 0:
+            arrived(at(zb, ft), base + 2, device(1))
+            go(at(zb, ft), at(zb, ft), base + 3, device(fy=True))
+            go(at(zb, ft), at(zb, ft), base + 4, device(fc=True))
+        elif k == 1:
+            arrived(at(zl, fy), base + 1, device(fy=True))
+            go(at(zl, fy), at(zl, fy), base + 5, device(fc=True))
+        else:
+            arrived(at(zb, fy), base + 3, device(fy=True))
+            go(at(zb, fy), at(zb, fy), base + 6, device(fc=True))
 
     def act_rest(name, at):
         base = sem_act[name]
@@ -648,20 +699,42 @@
         for k, b, f in ((0, zl, fc), (4, 1 - zl, fc), (5, zl, fyc), (6, 1 - zl, fyc)):
             arrived(at(b, f), base + k, device(fc=True))
 
+    def act_gathered(name, at):
+        base = sem_act[name]
+        fy = (1 - y) * 2 + c
+        zb = 1 - zl
+        to_c, to_y = device(fc=True), device(fy=True)
+        for k, b, f, where in (
+            (0, zl, ft, to_c),
+            (1, zl, ft, to_y),
+            (2, zl, ft, device(1)),
+            (3, zb, ft, to_y),
+            (4, zb, ft, to_c),
+            (5, zl, fy, to_c),
+            (6, zb, fy, to_c),
+        ):
+            send(at(b, f), at(b, f), base + k, where).wait_send()
+
     sem_z = {w: new(3) for w in ws}
     sem_x = {w: new(4) for w in ws}
 
-    def w_z(w):
-        for d in (3, 2, 1):
-            go(own_half(w, hl[d]), weight_at(w, dp), sem_z[w] + d - 1, device(d))
+    def w_z(w, d):
+        go(own_half(w, hl[d]), weight_at(w, dp), sem_z[w] + d - 1, device(d))
 
     def w_own(w):
         go(weight_at(w, dp), weight_at(w, dp), sem_x[w], device(fx=True))
 
     def w_forward(w, d):
-        block = zd[d] * 2 + x
-        arrived(weight_at(w, block), sem_z[w] + d - 1, device(d))
-        go(weight_at(w, block), weight_at(w, block), sem_x[w] + d, device(fx=True))
+        at = weight_at(w, partner(d) * 2 + x)
+        arrived(at, sem_z[w] + d - 1, device(d))
+        go(at, at, sem_x[w] + d, device(fx=True))
+
+    def w_sent(w):
+        for d in range(4):
+            at = weight_at(w, zd[d] * 2 + x)
+            send(at, at, sem_x[w] + d, device(fx=True)).wait_send()
+            if d > 0:
+                send(own_half(w, hl[d]), weight_at(w, dp), sem_z[w] + d - 1, device(d)).wait_send()
 
     def w_rest(w):
         for d in range(4):
@@ -676,16 +749,15 @@
         src, dst = m_["SX" + w].at[zp], m_["RX" + w].at[zp]
         send(src, dst, sem_gx[w] + zp, device(fx=True)).start()
 
-    def grad_z(w):
-        for d in (3, 2, 1, 0):
-            zp = zd[d]
-            arrived(m_["RX" + w].at[zp], sem_gx[w] + zp, device(fx=True))
-            both = m_["KX" + w][zp] + m_["RX" + w][zp].astype(f32)
-            if d == 0:
-                m_["KX" + w][zp] = both
-            else:
-                m_["ZS" + w][d - 1] = both.astype(bf16)
-                go(m_["ZS" + w].at[d - 1], m_["ZR" + w].at[d - 1], sem_gz[w] + d - 1, device(d))
+    def grad_z(w, d):
+        zp = zd[d]
+        arrived(m_["RX" + w].at[zp], sem_gx[w] + zp, device(fx=True))
+        both = m_["KX" + w][zp] + m_["RX" + w][zp].astype(f32)
+        if d == 0:
+            m_["KX" + w][zp] = both
+        else:
+            m_["ZS" + w][d - 1] = both.astype(bf16)
+            go(m_["ZS" + w].at[d - 1], m_["ZR" + w].at[d - 1], sem_gz[w] + d - 1, device(d))
 
     def grad_last(w):
         for d in (1, 2, 3):
@@ -693,20 +765,24 @@
         got = m_["ZR" + w]
         same = m_["KX" + w][z] + got[1].astype(f32)
         other = got[0].astype(f32) + got[2].astype(f32)
-        if w == "qkv":
+        if w == QKV:
             o_qkv[:, :, lanes(zl, s.half)] = same
             o_qkv[:, :, lanes(1 - zl, s.half)] = other
-        elif w == "up":
+        elif w == UP:
             o_up[:, lanes(zl, s.hidden)] = same
             o_up[:, lanes(1 - zl, s.hidden)] = other
-        elif w == "out":
+        elif w == OUT:
             o_out[lanes(zl, s.half), :] = same
             o_out[lanes(1 - zl, s.half), :] = other
         else:
             o_down[lanes(zl, s.hidden), :] = same
             o_down[lanes(1 - zl, s.hidden), :] = other
+
+    def grad_sent(w):
         for zp in range(4):
             send(m_["SX" + w].at[zp], m_["RX" + w].at[zp], sem_gx[w] + zp, device(fx=True)).wait_send()
+        for d in (1, 2, 3):
+            send(m_["ZS" + w].at[d - 1], m_["ZR" + w].at[d - 1], sem_gz[w] + d - 1, device(d)).wait_send()
 
     def pick(flag, a, b):
         return jnp.where(flag == 0, a, b)
@@ -716,9 +792,9 @@
         lo, hi = lax.slice_in_dim(value, 0, n, axis=axis), lax.slice_in_dim(value, n, 2 * n, axis=axis)
         return pick(x, lo, hi), pick(x, hi, lo)
 
-    sem_c = {k: new(4) for k in ("blk", "nrm")}
-    sem_y = {k: new(4) for k in ("blk", "nrm")}
-    sem_a = {k: new(2) for k in ("blk", "nrm")}
+    sem_c = {k: new(4) for k in (BLK, NRM)}
+    sem_y = {k: new(4) for k in (BLK, NRM)}
+    sem_a = {k: new(2) for k in (BLK, NRM)}
 
     def rows_of(i):
         block = (1 - zl) + (i // MB) * (2 * zl - 1)
@@ -768,14 +844,35 @@
             r = rows_of(i)
             send(m_["CS" + name].at[r], m_["CR" + name].at[r], sem_c[name] + i, device(fc=True)).wait_send()
             send(m_["YS" + name].at[r], m_["YR" + name].at[r], sem_y[name] + i, device(fy=True)).wait_send()
-
-    def loop(n, body):
-        lax.fori_loop(0, n, lambda i, carry: (body(i), carry)[1], 0)
+        for i in range(MB):
+            q = pl.ds(i * s.span, s.span)
+            send(m_["AS" + name].at[q], m_["AR" + name].at[q], sem_a[name] + i, device(1)).wait_send()
+
+    def beside(*steps):
+        def side(i):
+            for at in sorted(set(step[0] for step in steps)):
+
+                @pl.when(i == at)
+                def _():
+                    for when, do, *args in steps:
+                        if when == at:
+                            do(*args)
+
+        return side
+
+    def loop(n, body, side=None):
+        def step(i, carry):
+            if side is not None:
+                side(i)
+            body(i)
+            return carry
+
+        lax.fori_loop(0, n, step, 0)
 
     def at_micro(m):
         return pl.ds(mo(m * s.span, s.span), s.span)
 
-    def norm_phase():
+    def norm_phase(side=None):
         extra = XG[0, s.rows : s.rows + EXTRA, :].astype(f32)
         gain, shift = extra[0:1], extra[1:2]
 
@@ -789,7 +886,7 @@
             IV[r, :] = inv
             NB[r, :] = ((xv - mu) * inv * gain + shift).astype(bf16)
 
-        loop(s.micro, body)
+        loop(s.micro, body, side)
 
     def masks(m):
         extra = XG[m // MB, s.rows : s.rows + EXTRA, 0 : s.span].astype(f32)
@@ -820,7 +917,7 @@
         wide = dot(dot(dct[...], omega[...], precision=HIGHEST), rep[...], precision=HIGHEST)
         m_["A2"][...] = wide * (ones16[...].astype(f32) * (16.0 * HD ** (-0.25)))
 
-    def fwd_phase():
+    def fwd_phase(side=None):
         def body(m):
             r = at_micro(m)
             wq = jnp.concatenate([WQ[0], WQ[1], WQ[2]], 1)
@@ -857,9 +954,9 @@
             m_["ND"][r, :] = acc
             m_["AT"][r, :] = (acc[:, :hf] / acc[:, hf:]).astype(bf16)
 
-        loop(s.micro, body)
-
-    def bwd_phase():
+        loop(s.micro, body, side)
+
+    def bwd_phase(side=None):
         m_["QBG"][...] = jnp.zeros_like(m_["QBG"])
 
         def body(m):
@@ -894,9 +991,9 @@
             m_["PG"][r, :] = pg
             m_["QBG"][...] += jnp.sum(pg.astype(f32), 0, keepdims=True)
 
-        loop(s.micro, body)
-
-    def up_phase():
+        loop(s.micro, body, side)
+
+    def up_phase(side=None):
         bias = small[0:1, lanes(zl, s.hidden)]
 
         def body(m):
@@ -906,9 +1003,9 @@
             m_["HB"][r, :] = (pre * cdf).astype(bf16)
             m_["GP"][r, :] = cdf + pre * jnp.exp(-0.5 * pre * pre) * (1.0 / math.sqrt(2.0 * math.pi))
 
-        loop(s.micro, body)
-
-    def pre_phase():
+        loop(s.micro, body, side)
+
+    def pre_phase(side=None):
         m_["UBG"][...] = jnp.zeros_like(m_["UBG"])
 
         def body(m):
@@ -917,42 +1014,43 @@
             m_["PRE"][r, :] = pre
             m_["UBG"][...] += jnp.sum(pre.astype(f32), 0, keepdims=True)
 
-        loop(s.micro, body)
-
-    def nrm_phase():
+        loop(s.micro, body, side)
+
+    def nrm_phase(side=None):
         def body(i):
             r = rows_of(i)
             wq = jnp.concatenate([WQ[0], WQ[1], WQ[2]], 1)
-            act_put("nrm", i, dot(m_["PG"][r, :], wq, NT) + dot(m_["PRE"][r, :], WU[...], NT))
-
-        loop(4, body)
-
-    def blk_phase():
+            act_put(NRM, i, dot(m_["PG"][r, :], wq, NT) + dot(m_["PRE"][r, :], WU[...], NT))
+
+        loop(4, body, side)
+
+    def blk_phase(side=None):
         def body(i):
             r = rows_of(i)
-            act_put("blk", i, dot(m_["AT"][r, :], WO[...]) + dot(m_["HB"][r, :], WD[...]))
-
-        loop(4, body)
+            act_put(BLK, i, dot(m_["AT"][r, :], WO[...]) + dot(m_["HB"][r, :], WD[...]))
+
+        loop(4, body, side)
 
     two = 2 * s.block
 
-    def grad_phase(w):
-        def body(zp):
+    def grad_phase(w, side=None):
+        def body(i):
+            zp = partner(3 - i)
             cols = lanes(zp, two)
-            if w == "qkv":
+            if w == QKV:
                 value = dot(NB[:, cols], m_["PG"][...], TN)
                 mine, theirs = halves(value, 0)
                 mine = jnp.stack([mine[:, k * hf : (k + 1) * hf] for k in range(3)], 0)
                 theirs = jnp.stack([theirs[:, k * hf : (k + 1) * hf] for k in range(3)], 0)
-            elif w == "up":
+            elif w == UP:
                 mine, theirs = halves(dot(NB[:, cols], m_["PRE"][...], TN), 0)
-            elif w == "out":
+            elif w == OUT:
                 mine, theirs = halves(dot(m_["AT"][...], G[:, cols], TN), 1)
             else:
                 mine, theirs = halves(dot(m_["HB"][...], G[:, cols], TN), 1)
             put_grad(w, zp, mine, theirs)
 
-        loop(s.planes, body)
+        loop(s.planes, body, side)
 
     def out_rows(i):
         return pl.ds(i * s.span, s.span)
@@ -961,7 +1059,7 @@
         for i in range(MB):
             own = XG[zl, i * s.span : (i + 1) * s.span, lanes(ft, s.width)].astype(f32)
             bias = small[1:2, 3 * s.width : 4 * s.width]
-            o_blk[out_rows(i), :] = (own + act_last("blk", i) + bias).astype(bf16)
+            o_blk[out_rows(i), :] = (own + act_last(BLK, i) + bias).astype(bf16)
 
     sem_st = new(3)
     stat_where = [device(fc=True), device(fy=True), device(fy=True, fc=True)]
@@ -975,7 +1073,7 @@
 
     def nrm_last():
         for i in range(MB):
-            m_["NGF"][out_rows(i), :] = act_last("nrm", i)
+            m_["NGF"][out_rows(i), :] = act_last(NRM, i)
         gain, xhat = own_parts()
         ngrad = m_["NGF"][...]
         scaled = ngrad * gain
@@ -1028,68 +1126,157 @@
         inv = IV[lanes(zl, s.rows), :]
         o_inp[...] = (own_g + inv * (scaled - mean1 - xhat * mean2)).astype(bf16)
 
-    act_first("tok", tok_at)
-    w_own("qkv")
-    w_z("qkv")
-    w_own("out")
+    act_own(TOK, tok_at, "y")
+    act_own(TOK, tok_at, "z")
+    w_own(DOWN)
+    act_own(GRD, grd_at, "c")
+    w_z(QKV, 2)
+    w_own(QKV)
+    w_z(QKV, 1)
+    act_own(GRD, grd_at, "z")
+    act_own(GRD, grd_at, "y")
+    w_forward(QKV, 2)
+    w_forward(QKV, 1)
+    act_own(TOK, tok_at, "c")
+    act_arrive(TOK, tok_at, 0)
+    w_z(OUT, 2)
+    w_z(QKV, 3)
     table_phase()
-    act_forward("tok", tok_at)
-    act_first("grd", grd_at)
-    w_z("out")
-    w_z("up")
-    w_z("down")
-    for d in (1, 2, 3):
-        w_forward("qkv", d)
-    w_own("up")
-    w_own("down")
-    act_rest("tok", tok_at)
-    norm_phase()
-    act_forward("grd", grd_at)
-    for d in (1, 2, 3):
-        w_forward("out", d)
-    w_rest("qkv")
-    fwd_phase()
-    act_rest("grd", grd_at)
-    for d in (1, 2, 3):
-        w_forward("up", d)
-    w_rest("out")
-    bwd_phase()
-    grad_phase("out")
-    grad_phase("qkv")
-    for d in (1, 2, 3):
-        w_forward("down", d)
-    w_rest("up")
-    up_phase()
-    grad_z("out")
-    grad_z("qkv")
-    w_rest("down")
+    act_arrive(TOK, tok_at, 1)
+    w_own(OUT)
+    w_own(UP)
+    act_arrive(GRD, grd_at, 0)
+    act_arrive(TOK, tok_at, 2)
+    w_z(UP, 1)
+    w_forward(QKV, 3)
+    w_z(UP, 3)
+    w_z(OUT, 1)
+    act_rest(TOK, tok_at)
+    norm_phase(
+        beside(
+            (1, w_z, OUT, 3),
+        ),
+    )
+    w_forward(OUT, 2)
+    w_rest(QKV)
+    fwd_phase(
+        beside(
+            (1, w_forward, UP, 1),
+            (2, act_arrive, GRD, grd_at, 1),
+            (2, w_forward, UP, 3),
+            (2, w_z, UP, 2),
+            (2, w_forward, OUT, 1),
+            (2, act_arrive, GRD, grd_at, 2),
+        ),
+    )
+    w_forward(OUT, 3)
+    w_z(DOWN, 1)
+    act_rest(GRD, grd_at)
+    grad_phase(OUT)
+    w_z(DOWN, 3)
+    w_forward(UP, 2)
+    w_rest(OUT)
+    bwd_phase(
+        beside(
+            (2, w_z, DOWN, 2),
+            (2, w_forward, DOWN, 1),
+            (3, w_forward, DOWN, 3),
+        ),
+    )
+    grad_phase(
+        QKV,
+        beside(
+            (1, grad_z, OUT, 2),
+            (2, grad_z, OUT, 3),
+            (2, grad_z, OUT, 1),
+            (2, w_forward, DOWN, 2),
+        ),
+    )
+    w_rest(UP)
+    up_phase(
+        beside(
+            (1, grad_z, QKV, 3),
+        ),
+    )
+    grad_z(QKV, 2)
+    grad_phase(DOWN)
+    w_rest(DOWN)
+    blk_phase(
+        beside(
+            (3, act_y, BLK, 0),
+        ),
+    )
+    grad_z(QKV, 1)
     pre_phase()
-    nrm_phase()
-    blk_phase()
-    for i in range(4):
-        act_y("nrm", i)
-    grad_phase("up")
-    for i in range(4):
-        act_y("blk", i)
-    for i in range(2):
-        act_z("nrm", i)
-    grad_phase("down")
-    for i in range(2):
-        act_z("blk", i)
-    grad_z("up")
+    act_z(BLK, 0)
+    grad_z(DOWN, 3)
+    grad_z(OUT, 0)
+    act_y(BLK, 1)
+    nrm_phase(
+        beside(
+            (2, grad_last, OUT),
+        ),
+    )
+    act_y(NRM, 0)
+    grad_z(DOWN, 1)
+    grad_z(DOWN, 2)
+    grad_phase(
+        UP,
+        beside(
+            (2, act_y, NRM, 1),
+            (3, act_y, BLK, 3),
+            (3, act_z, NRM, 0),
+        ),
+    )
+    act_z(NRM, 1)
+    grad_z(UP, 2)
+    act_z(BLK, 1)
+    grad_z(DOWN, 0)
+    act_y(NRM, 3)
+    act_y(NRM, 2)
+    act_y(BLK, 2)
     nrm_last()
+    grad_z(UP, 1)
+    grad_z(UP, 0)
+    grad_z(QKV, 0)
+    grad_z(UP, 3)
+    grad_last(QKV)
     small_send()
-    grad_z("down")
+    input_last()
     blk_last()
-    input_last()
+    grad_last(DOWN)
+    grad_last(UP)
     small_last()
+    act_gathered(TOK, tok_at)
+    act_gathered(GRD, grd_at)
     for w in ws:
-        grad_last(w)
-    for copy in sent:
-        copy.wait_send()
-    for name in ("blk", "nrm"):
+        w_sent(w)
+        grad_sent(w)
+    for name in (BLK, NRM):
         act_sent(name)
+    for k, where in enumerate(stat_where):
+        send(m_["ST"], m_["STR"].at[k], sem_st + k, where).wait_send()
+    for k, where in enumerate(sv_where):
+        send(m_["SV"], m_["SVR"].at[k], sem_sv + k, where).wait_send()
     assert counter[0] <= N_REMOTE
+
+
+def finish_kernel(*refs):
+    whole, small = refs[:6], refs[6]
+    outs, (gain, shift, out_bias, qkv_bias, up_bias) = refs[7:13], refs[13:18]
+    sem = refs[18]
+    copies = [pltpu.make_async_copy(whole[i], outs[i], sem.at[i]) for i in range(6)]
+    for copy in copies:
+        copy.start()
+    for k, ref in enumerate((gain, shift, out_bias)):
+        ref[...] = small[2 * k : 2 * k + 2, :]
+    for k in range(3):
+        for j in range(2):
+            ref = qkv_bias.at[k : k + 1, j * 128 : (j + 1) * 128]
+            ref[...] = small[6 + 2 * k + j : 7 + 2 * k + j, :]
+    up_bias[...] = small[12 : 12 + up_bias.shape[0], :]
+    for copy in copies:
+        copy.wait()
 
 
 def on_device_fused(
@@ -1112,26 +1299,6 @@
 ):
     rows, width = tokens.shape
     s = Sizes(rows, width, up_weight.shape[1], dp_count, feat_count)
-    lens = jnp.broadcast_to(doc_lengths.reshape(-1, 1).astype(bf16), (doc_lengths.size, width))
-    extra = jnp.concatenate(
-        [
-            norm_gain[None],
-            norm_shift[None],
-            lens,
-            jnp.zeros((EXTRA - 2 - doc_lengths.size, width), bf16),
-        ],
-        0,
-    )
-    full = up_bias.shape[0]
-    lane_gain = jnp.concatenate([qmc_weights, qmc_weights, jnp.ones((width // 2,), f32)])
-    small = jnp.stack(
-        [
-            up_bias.astype(f32),
-            jnp.concatenate([qkv_bias.reshape(-1), out_bias]).astype(f32),
-            jnp.concatenate([lane_gain, jnp.zeros((full - lane_gain.shape[0],), f32)]),
-        ],
-        0,
-    )
     ones16 = np.kron(np.eye(4), np.full((HD, HD), 1.0 / 16.0)).astype(ml_dtypes.bfloat16)
     rep = np.tile(np.eye(HD, dtype=np.float32), (1, 4))
     shapes = scratch_list(s)
@@ -1142,34 +1309,40 @@
         pltpu.SemaphoreType.DMA((N_REMOTE,)),
         pltpu.SemaphoreType.DMA((N_REMOTE,)),
     ]
+    results = [
+        ((rows, width), bf16),
+        ((rows, width), bf16),
+        ((3, s.block, width), f32),
+        (up_weight.shape, f32),
+        (out_weight.shape, f32),
+        (down_weight.shape, f32),
+        ((24, 128), f32),
+    ]
     raw = pl.BlockSpec(memory_space=pl.ANY)
     vm = pl.BlockSpec(memory_space=pltpu.VMEM)
     outs = pl.pallas_call(
         functools.partial(fused_kernel, s, names),
-        out_shape=(
-            jax.ShapeDtypeStruct((rows, width), bf16),
-            jax.ShapeDtypeStruct((rows, width), bf16),
-            jax.ShapeDtypeStruct((3, s.block, width), f32),
-            jax.ShapeDtypeStruct(up_weight.shape, f32),
-            jax.ShapeDtypeStruct(out_weight.shape, f32),
-            jax.ShapeDtypeStruct(down_weight.shape, f32),
-            jax.ShapeDtypeStruct((24, 128), f32),
-        ),
-        in_specs=[raw] * 7 + [vm] * 7,
+        out_shape=tuple(pltpu.VMEM(shape, kind) for shape, kind in results),
+        in_specs=[raw] * (6 + len(SMALL)),
         out_specs=[vm] * 7,
         scratch_shapes=scratch,
         compiler_params=pltpu.CompilerParams(
-            collective_id=0, has_side_effects=True, vmem_limit_bytes=63 * 2**20
+            collective_id=0, has_side_effects=True, vmem_limit_bytes=56 * 2**20
         ),
     )(
         tokens,
         out_grad,
-        extra,
         jnp.transpose(qkv_weight, (1, 0, 2)),
         up_weight,
         out_weight,
         down_weight,
-        small,
+        doc_lengths,
+        norm_gain,
+        norm_shift,
+        qkv_bias,
+        out_bias,
+        up_bias,
+        qmc_weights,
         jnp.asarray(rotary_table(rows // MB // 2)),
         jnp.asarray(rotary_swap()),
         jnp.asarray(ones16),
@@ -1177,54 +1350,64 @@
         jnp.asarray(rep),
         omega,
     )
-    o_blk, o_inp, o_qkv, o_up, o_out, o_down, o_small = outs
-    flat = o_small.reshape(-1)
+    whole = [jax.ShapeDtypeStruct(shape, kind) for shape, kind in results[:6]]
+    full = up_bias.shape[0]
+    short = [(width // 128, 128)] * 3 + [(3, width), (full // 128, 128)]
+    done = pl.pallas_call(
+        finish_kernel,
+        out_shape=tuple(whole) + tuple(jax.ShapeDtypeStruct(shape, f32) for shape in short),
+        in_specs=[vm] * 7,
+        out_specs=[raw] * 6 + [vm] * 5,
+        scratch_shapes=[pltpu.SemaphoreType.DMA((6,))],
+        compiler_params=pltpu.CompilerParams(vmem_limit_bytes=4 * 2**20),
+    )(*(pltpu.with_memory_space_constraint(out, pltpu.VMEM) for out in outs))
+    o_blk, o_inp, o_qkv, o_up, o_out, o_down, gain, shift, out_bias_grad, qkv_bias_grad, up_bias_grad = done
     return (
         o_blk,
         o_inp,
-        flat[0:width],
-        flat[width : 2 * width],
+        gain.reshape(-1),
+        shift.reshape(-1),
         jnp.transpose(o_qkv, (1, 0, 2)),
-        flat[3 * width : 6 * width].reshape(3, width),
+        qkv_bias_grad,
         o_out,
-        flat[2 * width : 3 * width],
+        out_bias_grad.reshape(-1),
         o_up,
-        flat[6 * width : 6 * width + full],
+        up_bias_grad.reshape(-1),
         o_down,
     )
 
 
 def solution(mesh):
     in_specs = (
-        P("dp", "feat"),
-        P("dp", None),
-        P("feat"),
-        P("feat"),
-        P("dp", None, "feat"),
-        P(None, "feat"),
+        P(DP, FEAT),
+        P(DP, None),
+        P(FEAT),
+        P(FEAT),
+        P(DP, None, FEAT),
+        P(None, FEAT),
         P(),
         P(),
-        P("feat", "dp"),
-        P("feat"),
-        P("dp", "feat"),
-        P("feat"),
-        P("feat", "dp"),
-        P("dp", "feat"),
+        P(FEAT, DP),
+        P(FEAT),
+        P(DP, FEAT),
+        P(FEAT),
+        P(FEAT, DP),
+        P(DP, FEAT),
     )
     out_specs = (
-        P("dp", "feat"),
-        P("dp", "feat"),
-        P("feat"),
-        P("feat"),
-        P("dp", None, "feat"),
-        P(None, "feat"),
-        P("feat", "dp"),
-        P("feat"),
-        P("dp", "feat"),
-        P("feat"),
-        P("feat", "dp"),
-    )
-    dp_count, feat_count = mesh.shape["dp"], mesh.shape["feat"]
+        P(DP, FEAT),
+        P(DP, FEAT),
+        P(FEAT),
+        P(FEAT),
+        P(DP, None, FEAT),
+        P(None, FEAT),
+        P(FEAT, DP),
+        P(FEAT),
+        P(DP, FEAT),
+        P(FEAT),
+        P(FEAT, DP),
+    )
+    dp_count, feat_count = mesh.shape[DP], mesh.shape[FEAT]
     if (dp_count, feat_count) == (8, 4):
         per_device = functools.partial(on_device_fused, dp_count, feat_count)
     else:

time: 137 us -> 106 us (0.77)
  Pallas kernels: 122 us -> 105 us
  local copies, waits for them, and re-layouts: 12.7 us -> 0 us
  other arithmetic: 1.38 us -> 0 us
    pallas_call x1 -> x2, Pallas kernels: 122 us -> 105 us  [the longest x1 103 us: on_device_fused(): pl.pallas_call(functools.partial(fused_kernel, s, names), out_shape=tuple...]
    unnamed x33 -> x0, local copies, waits for them, and re-layouts: 10.7 us -> none
where the time goes in v2:
time: 106 us
  Pallas kernels  105 us (99%)
    pallas_call x1, Pallas kernels, on_device_fused(): pl.pallas_call(functools.partial(fused_kernel, s, names), out_shape=tuple...  103 us

profile of v2, /device:TPU:0, one launch (start us, length us, event | category | flops | bytes accessed | tf_op | source)
XLA Modules:
  0.0 105.5 jit_solution(8656381143169875696)
XLA Ops:
  0.6 102.9 %shard_map.266 = (bf16[512,256]{1,0:T(8,128)(2,1)S(1)}, bf16[512,256]{1,0:T(8,128)(2,1)S(1)}, f32[3,128,256]{2,1,0:T(8,128)S(1)}, f32[128,1024]{1,0:T(8,128)S(1)...) custom-call(bf16[512,256]{1,0:T(8,128)(2,1)} %refs_0_.1, bf16[512,256]{1,0:T(8,128)(2,1)} %refs_1_.1, ...), custom_call_target="tpu_custom_call" | custom-call | tf_op jit(solution)/shard_map/pallas_call | solution.py:1323
  103.5 2.0 %shard_map.267 = (bf16[512,256]{1,0:T(8,128)(2,1)}, bf16[512,256]{1,0:T(8,128)(2,1)}, f32[3,128,256]{2,1,0:T(8,128)}, f32[128,1024]{1,0:T(8,128)}, f32[256,128]{...) custom-call(bf16[512,256]{1,0:T(8,128)(2,1)S(1)} %get-tuple-element., ...), custom_call_target="tpu_custom_call" | custom-call | tf_op jit(solution)/shard_map/pallas_call | solution.py:1356

commit v3 on v2

--- a/solution.py
+++ b/solution.py
@@ -532,6 +532,7 @@
         shapes["KX" + name] = ((pl_,) + shape, f32)
         shapes["ZS" + name] = ((3,) + shape, bf16)
         shapes["ZR" + name] = ((3,) + shape, bf16)
+        shapes["ZM" + name] = (shape, bf16)
     for name in (BLK, NRM):
         shapes["CS" + name] = ((tt, 2 * s.width), bf16)
         shapes["CR" + name] = ((tt, 2 * s.width), bf16)
@@ -567,6 +568,7 @@
     y, c = ft // 2, ft % 2
     zd = (z, z + 1 - 2 * zl, (z + 2) % 4, 3 - z)
     hl = (zl, 1 - zl, zl, 1 - zl)
+    inner = zl != z // 2
 
     def partner(d):
         if isinstance(d, int):
@@ -585,12 +587,12 @@
             FEAT: (1 - y if fy else y) * 2 + (1 - c if fc else c),
         }
 
-    def send(src, dst, sem, where):
+    def send(src, dst, sem, where, arrival=None):
         copy = pltpu.make_async_remote_copy(
             src_ref=src,
             dst_ref=dst,
             send_sem=ssem.at[sem],
-            recv_sem=rsem.at[sem],
+            recv_sem=rsem.at[sem if arrival is None else arrival],
             device_id=where,
             device_id_type=MESH,
         )
@@ -650,7 +652,8 @@
     for where in partners:
         pl.semaphore_signal(barrier, inc=1, device_id=where, device_id_type=MESH)
     pl.semaphore_wait(barrier, len(partners))
-    for copy in local:
+    local_grd, local_weight, local_table = local[1], dict(zip(ws, local[2:6])), local[-6:]
+    for copy in local[:1] + local[6:-6]:
         copy.wait()
 
     def row_of(name):
@@ -675,7 +678,7 @@
 
     def act_own(name, at, axis):
         k, where = {"c": (0, device(fc=True)), "y": (1, device(fy=True)), "z": (2, device(1))}[axis]
-        go(at(zl, ft), at(zl, ft), sem_act[name] + k, where)
+        go(at(zl, ft) if name == TOK else grd, at(zl, ft), sem_act[name] + k, where)
 
     def act_arrive(name, at, k):
         base = sem_act[name]
@@ -694,6 +697,8 @@
 
     def act_rest(name, at):
         base = sem_act[name]
+        if name == GRD:
+            local_grd.wait()
         fc = y * 2 + 1 - c
         fyc = (1 - y) * 2 + 1 - c
         for k, b, f in ((0, zl, fc), (4, 1 - zl, fc), (5, zl, fyc), (6, 1 - zl, fyc)):
@@ -717,26 +722,66 @@
 
     sem_z = {w: new(3) for w in ws}
     sem_x = {w: new(4) for w in ws}
+    sem_r = {w: new() for w in ws}
+    sem_m = {w: new() for w in ws}
+
+    waited = set()
 
     def w_z(w, d):
-        go(own_half(w, hl[d]), weight_at(w, dp), sem_z[w] + d - 1, device(d))
+        def start():
+            go(own_half(w, hl[d]), weight_at(w, dp), sem_z[w] + d - 1, device(d))
+
+        if d == 3:
+            pl.when(inner)(start)
+        else:
+            start()
+
+    def w_near(w):
+        at = weight_at(w, zd[1] * 2 + x)
+        arrived(at, sem_z[w], device(1))
+
+    def relay(w):
+        at = weight_at(w, zd[1] * 2 + x)
+        return send(at, at, sem_r[w], device(2), sem_z[w] + 2)
+
+    def w_relay(w):
+        first = w not in waited
+        waited.add(w)
+
+        @pl.when(inner)
+        def _():
+            if first:
+                w_near(w)
+            relay(w).start()
 
     def w_own(w):
-        go(weight_at(w, dp), weight_at(w, dp), sem_x[w], device(fx=True))
+        go(own_half(w, zl), weight_at(w, dp), sem_x[w], device(fx=True))
 
     def w_forward(w, d):
         at = weight_at(w, partner(d) * 2 + x)
-        arrived(at, sem_z[w] + d - 1, device(d))
+        if d > 1:
+            arrived(at, sem_z[w] + d - 1, device(d))
+        elif w in waited:
+            pl.when(jnp.logical_not(inner))(lambda: w_near(w))
+        else:
+            waited.add(w)
+            w_near(w)
         go(at, at, sem_x[w] + d, device(fx=True))
 
     def w_sent(w):
         for d in range(4):
             at = weight_at(w, zd[d] * 2 + x)
             send(at, at, sem_x[w] + d, device(fx=True)).wait_send()
-            if d > 0:
+            if d in (1, 2):
                 send(own_half(w, hl[d]), weight_at(w, dp), sem_z[w] + d - 1, device(d)).wait_send()
 
+        @pl.when(inner)
+        def _():
+            send(own_half(w, hl[3]), weight_at(w, dp), sem_z[w] + 2, device(3)).wait_send()
+            relay(w).wait_send()
+
     def w_rest(w):
+        local_weight[w].wait()
         for d in range(4):
             arrived(weight_at(w, zd[d] * 2 + 1 - x), sem_x[w] + d, device(fx=True))
 
@@ -748,6 +793,12 @@
         m_["SX" + w][zp] = theirs.astype(bf16)
         src, dst = m_["SX" + w].at[zp], m_["RX" + w].at[zp]
         send(src, dst, sem_gx[w] + zp, device(fx=True)).start()
+
+    def grad_copy(w, d):
+        return send(m_["ZS" + w].at[d - 1], m_["ZR" + w].at[d - 1], sem_gz[w] + d - 1, device(d))
+
+    def grad_pass(w):
+        return send(m_["ZS" + w].at[2], m_["ZM" + w], sem_m[w], device(2))
 
     def grad_z(w, d):
         zp = zd[d]
@@ -755,34 +806,58 @@
         both = m_["KX" + w][zp] + m_["RX" + w][zp].astype(f32)
         if d == 0:
             m_["KX" + w][zp] = both
+            return
+        if d == 1:
+
+            @pl.when(inner)
+            def _():
+                arrived(m_["ZM" + w], sem_m[w], device(2))
+                m_["ZS" + w][0] = (both + m_["ZM" + w][...].astype(f32)).astype(bf16)
+
+            @pl.when(jnp.logical_not(inner))
+            def _():
+                m_["ZS" + w][0] = both.astype(bf16)
+
         else:
             m_["ZS" + w][d - 1] = both.astype(bf16)
-            go(m_["ZS" + w].at[d - 1], m_["ZR" + w].at[d - 1], sem_gz[w] + d - 1, device(d))
+        if d < 3:
+            grad_copy(w, d).start()
+        else:
+            pl.when(inner)(lambda: grad_copy(w, 3).start())
+            pl.when(jnp.logical_not(inner))(lambda: grad_pass(w).start())
 
     def grad_last(w):
-        for d in (1, 2, 3):
+        for d in (1, 2):
             arrived(m_["ZR" + w].at[d - 1], sem_gz[w] + d - 1, device(d))
         got = m_["ZR" + w]
         same = m_["KX" + w][z] + got[1].astype(f32)
-        other = got[0].astype(f32) + got[2].astype(f32)
-        if w == QKV:
-            o_qkv[:, :, lanes(zl, s.half)] = same
-            o_qkv[:, :, lanes(1 - zl, s.half)] = other
-        elif w == UP:
-            o_up[:, lanes(zl, s.hidden)] = same
-            o_up[:, lanes(1 - zl, s.hidden)] = other
-        elif w == OUT:
-            o_out[lanes(zl, s.half), :] = same
-            o_out[lanes(1 - zl, s.half), :] = other
-        else:
-            o_down[lanes(zl, s.hidden), :] = same
-            o_down[lanes(1 - zl, s.hidden), :] = other
+        other = got[0].astype(f32)
+        def put(half, value):
+            if w == QKV:
+                o_qkv[:, :, lanes(half, s.half)] = value
+            elif w == UP:
+                o_up[:, lanes(half, s.hidden)] = value
+            elif w == OUT:
+                o_out[lanes(half, s.half), :] = value
+            else:
+                o_down[lanes(half, s.hidden), :] = value
+
+        put(zl, same)
+
+        @pl.when(inner)
+        def _():
+            arrived(m_["ZR" + w].at[2], sem_gz[w] + 2, device(3))
+            put(1 - zl, other + got[2].astype(f32))
+
+        pl.when(jnp.logical_not(inner))(lambda: put(1 - zl, other))
 
     def grad_sent(w):
         for zp in range(4):
             send(m_["SX" + w].at[zp], m_["RX" + w].at[zp], sem_gx[w] + zp, device(fx=True)).wait_send()
-        for d in (1, 2, 3):
-            send(m_["ZS" + w].at[d - 1], m_["ZR" + w].at[d - 1], sem_gz[w] + d - 1, device(d)).wait_send()
+        for d in (1, 2):
+            grad_copy(w, d).wait_send()
+        pl.when(inner)(lambda: grad_copy(w, 3).wait_send())
+        pl.when(jnp.logical_not(inner))(lambda: grad_pass(w).wait_send())
 
     def pick(flag, a, b):
         return jnp.where(flag == 0, a, b)
@@ -914,6 +989,8 @@
     hf = s.half
 
     def table_phase():
+        for copy in local_table:
+            copy.wait()
         wide = dot(dot(dct[...], omega[...], precision=HIGHEST), rep[...], precision=HIGHEST)
         m_["A2"][...] = wide * (ones16[...].astype(f32) * (16.0 * HD ** (-0.25)))
 
@@ -1126,125 +1203,140 @@
         inv = IV[lanes(zl, s.rows), :]
         o_inp[...] = (own_g + inv * (scaled - mean1 - xhat * mean2)).astype(bf16)
 
+    w_z(QKV, 3)
+    w_z(QKV, 1)
+    act_own(GRD, grd_at, "y")
+    table_phase()
+    w_own(DOWN)
+    act_own(TOK, tok_at, "c")
+    w_own(QKV)
     act_own(TOK, tok_at, "y")
+    w_z(OUT, 3)
+    w_own(UP)
+    w_z(OUT, 1)
     act_own(TOK, tok_at, "z")
-    w_own(DOWN)
-    act_own(GRD, grd_at, "c")
+    w_z(UP, 3)
+    w_relay(QKV)
+    act_own(GRD, grd_at, "z")
+    w_forward(OUT, 1)
     w_z(QKV, 2)
-    w_own(QKV)
-    w_z(QKV, 1)
-    act_own(GRD, grd_at, "z")
-    act_own(GRD, grd_at, "y")
-    w_forward(QKV, 2)
-    w_forward(QKV, 1)
-    act_own(TOK, tok_at, "c")
+    w_z(OUT, 2)
     act_arrive(TOK, tok_at, 0)
-    w_z(OUT, 2)
-    w_z(QKV, 3)
-    table_phase()
+    w_z(DOWN, 1)
     act_arrive(TOK, tok_at, 1)
     w_own(OUT)
-    w_own(UP)
+    w_forward(QKV, 1)
+    w_forward(QKV, 3)
+    w_forward(QKV, 2)
+    act_own(GRD, grd_at, "c")
+    act_arrive(TOK, tok_at, 2)
     act_arrive(GRD, grd_at, 0)
-    act_arrive(TOK, tok_at, 2)
     w_z(UP, 1)
-    w_forward(QKV, 3)
-    w_z(UP, 3)
-    w_z(OUT, 1)
     act_rest(TOK, tok_at)
+    w_relay(OUT)
+    w_forward(OUT, 2)
+    w_z(DOWN, 3)
     norm_phase(
         beside(
-            (1, w_z, OUT, 3),
+            (3, w_forward, OUT, 3),
         ),
     )
-    w_forward(OUT, 2)
+    w_z(UP, 2)
     w_rest(QKV)
     fwd_phase(
         beside(
-            (1, w_forward, UP, 1),
-            (2, act_arrive, GRD, grd_at, 1),
-            (2, w_forward, UP, 3),
-            (2, w_z, UP, 2),
-            (2, w_forward, OUT, 1),
-            (2, act_arrive, GRD, grd_at, 2),
+            (1, w_forward, DOWN, 1),
+            (1, act_arrive, GRD, grd_at, 1),
+            (2, w_forward, UP, 1),
+            (3, act_arrive, GRD, grd_at, 2),
         ),
     )
-    w_forward(OUT, 3)
-    w_z(DOWN, 1)
     act_rest(GRD, grd_at)
-    grad_phase(OUT)
-    w_z(DOWN, 3)
+    grad_phase(
+        OUT,
+        beside(
+            (2, w_rest, OUT),
+            (2, w_relay, DOWN),
+        ),
+    )
     w_forward(UP, 2)
-    w_rest(OUT)
     bwd_phase(
         beside(
-            (2, w_z, DOWN, 2),
-            (2, w_forward, DOWN, 1),
-            (3, w_forward, DOWN, 3),
+            (1, w_forward, DOWN, 3),
+            (1, w_relay, UP),
+            (1, w_z, DOWN, 2),
+            (3, w_forward, UP, 3),
         ),
     )
     grad_phase(
         QKV,
         beside(
+            (1, w_forward, DOWN, 2),
             (1, grad_z, OUT, 2),
+            (2, w_rest, UP),
             (2, grad_z, OUT, 3),
-            (2, grad_z, OUT, 1),
-            (2, w_forward, DOWN, 2),
         ),
     )
-    w_rest(UP)
     up_phase(
         beside(
             (1, grad_z, QKV, 3),
         ),
     )
-    grad_z(QKV, 2)
-    grad_phase(DOWN)
+    grad_z(OUT, 1)
     w_rest(DOWN)
     blk_phase(
         beside(
-            (3, act_y, BLK, 0),
+            (1, grad_z, OUT, 0),
+            (3, grad_z, QKV, 2),
         ),
     )
-    grad_z(QKV, 1)
-    pre_phase()
-    act_z(BLK, 0)
-    grad_z(DOWN, 3)
-    grad_z(OUT, 0)
     act_y(BLK, 1)
+    grad_phase(
+        DOWN,
+        beside(
+            (1, act_y, BLK, 0),
+            (1, grad_last, OUT),
+            (2, grad_z, QKV, 1),
+        ),
+    )
+    act_z(BLK, 1)
+    pre_phase(
+        beside(
+            (1, grad_z, DOWN, 3),
+            (3, act_z, BLK, 0),
+        ),
+    )
     nrm_phase(
         beside(
-            (2, grad_last, OUT),
+            (2, act_y, NRM, 0),
+            (3, grad_z, DOWN, 2),
         ),
     )
-    act_y(NRM, 0)
-    grad_z(DOWN, 1)
-    grad_z(DOWN, 2)
+    grad_z(QKV, 0)
+    grad_z(DOWN, 0)
+    act_y(NRM, 1)
+    act_z(NRM, 0)
+    act_y(NRM, 2)
     grad_phase(
         UP,
         beside(
-            (2, act_y, NRM, 1),
-            (3, act_y, BLK, 3),
-            (3, act_z, NRM, 0),
+            (1, act_y, BLK, 3),
+            (1, grad_z, DOWN, 1),
+            (3, grad_z, UP, 3),
         ),
     )
     act_z(NRM, 1)
+    grad_last(DOWN)
+    act_y(BLK, 2)
+    grad_last(QKV)
+    act_y(NRM, 3)
     grad_z(UP, 2)
-    act_z(BLK, 1)
-    grad_z(DOWN, 0)
-    act_y(NRM, 3)
-    act_y(NRM, 2)
-    act_y(BLK, 2)
+    grad_z(UP, 0)
+    grad_z(UP, 1)
+    blk_last()
     nrm_last()
-    grad_z(UP, 1)
-    grad_z(UP, 0)
-    grad_z(QKV, 0)
-    grad_z(UP, 3)
-    grad_last(QKV)
     small_send()
     input_last()
-    blk_last()
-    grad_last(DOWN)
     grad_last(UP)
     small_last()
     act_gathered(TOK, tok_at)

time: 106 us -> 101 us (0.953)
  Pallas kernels: 105 us -> 101 us
    pallas_call x1, Pallas kernels: 103 us -> 98.6 us  [on_device_fused(): pl.pallas_call(functools.partial(fused_kernel, s, names), out_shape=tuple...]
where the time goes in v3:
time: 101 us
  Pallas kernels  101 us (100%)
    pallas_call x1, Pallas kernels, on_device_fused(): pl.pallas_call(functools.partial(fused_kernel, s, names), out_shape=tuple...  98.6 us

profile of v3, /device:TPU:0, one launch (start us, length us, event | category | flops | bytes accessed | tf_op | source)
XLA Modules:
  0.0 101.2 jit_solution(13855149383675349073)
XLA Ops:
  0.6 98.6 %shard_map.266 = (bf16[512,256]{1,0:T(8,128)(2,1)S(1)}, bf16[512,256]{1,0:T(8,128)(2,1)S(1)}, f32[3,128,256]{2,1,0:T(8,128)S(1)}, f32[128,1024]{1,0:T(8,128)S(1)...) custom-call(bf16[512,256]{1,0:T(8,128)(2,1)} %refs_0_.1, bf16[512,256]{1,0:T(8,128)(2,1)} %refs_1_.1, ...), custom_call_target="tpu_custom_call" | custom-call | tf_op jit(solution)/shard_map/pallas_call | solution.py:1415
  99.3 2.0 %shard_map.267 = (bf16[512,256]{1,0:T(8,128)(2,1)}, bf16[512,256]{1,0:T(8,128)(2,1)}, f32[3,128,256]{2,1,0:T(8,128)}, f32[128,1024]{1,0:T(8,128)}, f32[256,128]{...) custom-call(bf16[512,256]{1,0:T(8,128)(2,1)S(1)} %get-tuple-element., ...), custom_call_target="tpu_custom_call" | custom-call | tf_op jit(solution)/shard_map/pallas_call | solution.py:1448

commit v4 on v3

--- a/solution.py
+++ b/solution.py
@@ -1203,149 +1203,140 @@
         inv = IV[lanes(zl, s.rows), :]
         o_inp[...] = (own_g + inv * (scaled - mean1 - xhat * mean2)).astype(bf16)
 
+    act_own(TOK, tok_at, "z")
+    act_own(GRD, grd_at, "y")
+    w_z(QKV, 1)
+    w_own(DOWN)
+    w_z(OUT, 2)
     w_z(QKV, 3)
-    w_z(QKV, 1)
-    act_own(GRD, grd_at, "y")
-    table_phase()
-    w_own(DOWN)
+    w_z(OUT, 3)
+    w_z(QKV, 2)
+    w_own(OUT)
+    act_own(TOK, tok_at, "y")
+    w_own(UP)
+    act_own(GRD, grd_at, "z")
     act_own(TOK, tok_at, "c")
+    act_own(GRD, grd_at, "c")
+    w_forward(OUT, 2)
+    w_relay(QKV)
+    w_z(UP, 3)
+    w_forward(QKV, 1)
+    act_arrive(TOK, tok_at, 0)
+    act_arrive(TOK, tok_at, 1)
     w_own(QKV)
-    act_own(TOK, tok_at, "y")
-    w_z(OUT, 3)
-    w_own(UP)
+    w_forward(QKV, 3)
     w_z(OUT, 1)
-    act_own(TOK, tok_at, "z")
-    w_z(UP, 3)
-    w_relay(QKV)
-    act_own(GRD, grd_at, "z")
-    w_forward(OUT, 1)
-    w_z(QKV, 2)
-    w_z(OUT, 2)
-    act_arrive(TOK, tok_at, 0)
+    w_z(UP, 2)
+    w_relay(OUT)
     w_z(DOWN, 1)
-    act_arrive(TOK, tok_at, 1)
-    w_own(OUT)
-    w_forward(QKV, 1)
-    w_forward(QKV, 3)
+    act_arrive(TOK, tok_at, 2)
     w_forward(QKV, 2)
-    act_own(GRD, grd_at, "c")
-    act_arrive(TOK, tok_at, 2)
+    w_z(DOWN, 3)
+    act_arrive(GRD, grd_at, 1)
     act_arrive(GRD, grd_at, 0)
     w_z(UP, 1)
+    table_phase()
     act_rest(TOK, tok_at)
-    w_relay(OUT)
-    w_forward(OUT, 2)
-    w_z(DOWN, 3)
     norm_phase(
         beside(
-            (3, w_forward, OUT, 3),
+            (1, w_forward, OUT, 1),
         ),
     )
-    w_z(UP, 2)
+    w_forward(UP, 2)
     w_rest(QKV)
     fwd_phase(
         beside(
-            (1, w_forward, DOWN, 1),
-            (1, act_arrive, GRD, grd_at, 1),
-            (2, w_forward, UP, 1),
+            (2, w_forward, OUT, 3),
+            (2, w_forward, DOWN, 1),
             (3, act_arrive, GRD, grd_at, 2),
+            (3, w_relay, DOWN),
+            (3, w_relay, UP),
+            (3, w_forward, UP, 1),
+            (3, w_rest, OUT),
+            (3, w_z, DOWN, 2),
         ),
     )
     act_rest(GRD, grd_at)
-    grad_phase(
-        OUT,
-        beside(
-            (2, w_rest, OUT),
-            (2, w_relay, DOWN),
-        ),
-    )
-    w_forward(UP, 2)
     bwd_phase(
         beside(
             (1, w_forward, DOWN, 3),
-            (1, w_relay, UP),
-            (1, w_z, DOWN, 2),
             (3, w_forward, UP, 3),
         ),
     )
+    w_forward(DOWN, 2)
     grad_phase(
         QKV,
         beside(
-            (1, w_forward, DOWN, 2),
-            (1, grad_z, OUT, 2),
-            (2, w_rest, UP),
-            (2, grad_z, OUT, 3),
+            (3, w_rest, UP),
         ),
     )
-    up_phase(
-        beside(
-            (1, grad_z, QKV, 3),
-        ),
-    )
-    grad_z(OUT, 1)
+    up_phase()
     w_rest(DOWN)
     blk_phase(
         beside(
-            (1, grad_z, OUT, 0),
-            (3, grad_z, QKV, 2),
+            (2, grad_z, QKV, 3),
         ),
     )
+    act_y(BLK, 0)
+    grad_z(QKV, 2)
+    grad_phase(DOWN)
     act_y(BLK, 1)
-    grad_phase(
-        DOWN,
-        beside(
-            (1, act_y, BLK, 0),
-            (1, grad_last, OUT),
-            (2, grad_z, QKV, 1),
-        ),
-    )
-    act_z(BLK, 1)
+    grad_z(QKV, 1)
     pre_phase(
         beside(
-            (1, grad_z, DOWN, 3),
-            (3, act_z, BLK, 0),
+            (2, act_z, BLK, 0),
+            (3, grad_z, DOWN, 3),
         ),
     )
     nrm_phase(
         beside(
-            (2, act_y, NRM, 0),
-            (3, grad_z, DOWN, 2),
+            (2, act_z, BLK, 1),
+            (3, act_y, NRM, 0),
         ),
     )
-    grad_z(QKV, 0)
-    grad_z(DOWN, 0)
     act_y(NRM, 1)
-    act_z(NRM, 0)
-    act_y(NRM, 2)
+    grad_z(DOWN, 2)
+    grad_phase(OUT)
+    grad_z(DOWN, 1)
     grad_phase(
         UP,
         beside(
-            (1, act_y, BLK, 3),
-            (1, grad_z, DOWN, 1),
-            (3, grad_z, UP, 3),
+            (1, act_y, NRM, 2),
+            (1, act_z, NRM, 0),
+            (1, act_y, NRM, 3),
+            (3, grad_z, QKV, 0),
         ),
     )
     act_z(NRM, 1)
-    grad_last(DOWN)
+    grad_z(OUT, 3)
+    grad_z(UP, 3)
+    grad_z(UP, 2)
+    grad_last(QKV)
+    act_y(BLK, 3)
+    grad_z(OUT, 1)
     act_y(BLK, 2)
-    grad_last(QKV)
-    act_y(NRM, 3)
-    grad_z(UP, 2)
-    grad_z(UP, 0)
     grad_z(UP, 1)
-    blk_last()
-    nrm_last()
-    small_send()
-    input_last()
-    grad_last(UP)
-    small_last()
     act_gathered(TOK, tok_at)
     act_gathered(GRD, grd_at)
     for w in ws:
         w_sent(w)
+    nrm_last()
+    small_send()
+    grad_z(UP, 0)
+    blk_last()
+    grad_z(OUT, 0)
+    grad_z(DOWN, 0)
+    grad_z(OUT, 2)
+    grad_last(DOWN)
+    input_last()
+    grad_last(UP)
+    for w in (QKV, OUT, DOWN):
         grad_sent(w)
     for name in (BLK, NRM):
         act_sent(name)
+    small_last()
+    grad_last(OUT)
+    grad_sent(UP)
     for k, where in enumerate(stat_where):
         send(m_["ST"], m_["STR"].at[k], sem_st + k, where).wait_send()
     for k, where in enumerate(sv_where):

time: 101 us -> 100 us (0.990)
  Pallas kernels: 101 us -> 99.2 us
    pallas_call x1, Pallas kernels: 98.6 us -> 97.2 us  [on_device_fused(): pl.pallas_call(functools.partial(fused_kernel, s, names), out_shape=tuple...]
where the time goes in v4:
time: 100 us; the launch traced here: 99.9 us
  Pallas kernels  99.2 us (99%)
    pallas_call x1, Pallas kernels, on_device_fused(): pl.pallas_call(functools.partial(fused_kernel, s, names), out_shape=tuple...  97.2 us

profile of v4, /device:TPU:0, one launch (start us, length us, event | category | flops | bytes accessed | tf_op | source)
XLA Modules:
  0.0 99.9 jit_solution(3748855238561448430)
XLA Ops:
  0.6 97.2 %shard_map.266 = (bf16[512,256]{1,0:T(8,128)(2,1)S(1)}, bf16[512,256]{1,0:T(8,128)(2,1)S(1)}, f32[3,128,256]{2,1,0:T(8,128)S(1)}, f32[128,1024]{1,0:T(8,128)S(1)...) custom-call(bf16[512,256]{1,0:T(8,128)(2,1)} %refs_0_.1, bf16[512,256]{1,0:T(8,128)(2,1)} %refs_1_.1, ...), custom_call_target="tpu_custom_call" | custom-call | tf_op jit(solution)/shard_map/pallas_call | solution.py:1406
  97.9 2.0 %shard_map.267 = (bf16[512,256]{1,0:T(8,128)(2,1)}, bf16[512,256]{1,0:T(8,128)(2,1)}, f32[3,128,256]{2,1,0:T(8,128)}, f32[128,1024]{1,0:T(8,128)}, f32[256,128]{...) custom-call(bf16[512,256]{1,0:T(8,128)(2,1)S(1)} %get-tuple-element., ...), custom_call_target="tpu_custom_call" | custom-call | tf_op jit(solution)/shard_map/pallas_call | solution.py:1439

commit v5 on v4

--- a/solution.py
+++ b/solution.py
@@ -1203,139 +1203,146 @@
         inv = IV[lanes(zl, s.rows), :]
         o_inp[...] = (own_g + inv * (scaled - mean1 - xhat * mean2)).astype(bf16)
 
+    w_z(OUT, 3)
     act_own(TOK, tok_at, "z")
-    act_own(GRD, grd_at, "y")
-    w_z(QKV, 1)
-    w_own(DOWN)
-    w_z(OUT, 2)
-    w_z(QKV, 3)
-    w_z(OUT, 3)
-    w_z(QKV, 2)
+    w_own(QKV)
     w_own(OUT)
     act_own(TOK, tok_at, "y")
+    w_z(DOWN, 3)
+    w_z(OUT, 1)
+    act_own(TOK, tok_at, "c")
+    w_z(QKV, 2)
     w_own(UP)
+    w_relay(OUT)
+    act_arrive(TOK, tok_at, 1)
+    w_z(DOWN, 1)
+    act_arrive(TOK, tok_at, 0)
+    w_z(QKV, 3)
+    act_own(GRD, grd_at, "y")
+    w_own(DOWN)
+    w_forward(QKV, 2)
+    w_z(QKV, 1)
+    w_z(UP, 1)
+    w_forward(OUT, 3)
+    w_z(UP, 3)
+    w_forward(DOWN, 1)
+    w_forward(OUT, 1)
     act_own(GRD, grd_at, "z")
-    act_own(TOK, tok_at, "c")
+    w_z(UP, 2)
+    w_relay(QKV)
+    w_forward(QKV, 1)
+    act_arrive(TOK, tok_at, 2)
+    w_forward(UP, 1)
+    w_forward(QKV, 3)
+    act_rest(TOK, tok_at)
+    w_z(OUT, 2)
+    table_phase()
+    w_forward(UP, 2)
     act_own(GRD, grd_at, "c")
-    w_forward(OUT, 2)
-    w_relay(QKV)
-    w_z(UP, 3)
-    w_forward(QKV, 1)
-    act_arrive(TOK, tok_at, 0)
-    act_arrive(TOK, tok_at, 1)
-    w_own(QKV)
-    w_forward(QKV, 3)
-    w_z(OUT, 1)
-    w_z(UP, 2)
-    w_relay(OUT)
-    w_z(DOWN, 1)
-    act_arrive(TOK, tok_at, 2)
-    w_forward(QKV, 2)
-    w_z(DOWN, 3)
     act_arrive(GRD, grd_at, 1)
+    w_relay(UP)
+    w_z(DOWN, 2)
     act_arrive(GRD, grd_at, 0)
-    w_z(UP, 1)
-    table_phase()
-    act_rest(TOK, tok_at)
     norm_phase(
         beside(
-            (1, w_forward, OUT, 1),
+            (1, w_forward, OUT, 2),
+            (1, w_rest, QKV),
+            (2, w_relay, DOWN),
         ),
     )
-    w_forward(UP, 2)
-    w_rest(QKV)
     fwd_phase(
         beside(
-            (2, w_forward, OUT, 3),
-            (2, w_forward, DOWN, 1),
-            (3, act_arrive, GRD, grd_at, 2),
-            (3, w_relay, DOWN),
-            (3, w_relay, UP),
-            (3, w_forward, UP, 1),
-            (3, w_rest, OUT),
-            (3, w_z, DOWN, 2),
+            (1, w_forward, UP, 3),
+            (3, w_forward, DOWN, 2),
         ),
     )
-    act_rest(GRD, grd_at)
+    act_arrive(GRD, grd_at, 2)
+    w_rest(UP)
+    up_phase(
+        beside(
+            (1, w_forward, DOWN, 3),
+            (3, act_rest, GRD, grd_at),
+        ),
+    )
+    grad_phase(DOWN)
+    w_rest(DOWN)
+    pre_phase(
+        beside(
+            (1, w_rest, OUT),
+        ),
+    )
+    blk_phase(
+        beside(
+            (1, grad_z, DOWN, 3),
+        ),
+    )
+    act_y(BLK, 0)
+    grad_phase(
+        UP,
+        beside(
+            (1, grad_z, DOWN, 2),
+            (2, act_y, BLK, 1),
+        ),
+    )
+    act_y(BLK, 2)
+    grad_z(DOWN, 1)
+    act_z(BLK, 0)
     bwd_phase(
         beside(
-            (1, w_forward, DOWN, 3),
-            (3, w_forward, UP, 3),
+            (2, grad_z, UP, 3),
+            (3, act_z, BLK, 1),
         ),
     )
-    w_forward(DOWN, 2)
+    nrm_phase(
+        beside(
+            (2, grad_z, UP, 2),
+            (3, act_y, NRM, 0),
+        ),
+    )
+    grad_z(UP, 1)
+    grad_phase(
+        OUT,
+        beside(
+            (1, act_y, NRM, 1),
+            (3, act_y, NRM, 2),
+        ),
+    )
     grad_phase(
         QKV,
         beside(
-            (3, w_rest, UP),
+            (2, grad_z, OUT, 3),
+            (2, act_z, NRM, 0),
+            (2, grad_z, UP, 0),
+            (2, act_y, NRM, 3),
+            (2, act_z, NRM, 1),
+            (3, grad_z, QKV, 3),
         ),
     )
-    up_phase()
-    w_rest(DOWN)
-    blk_phase(
-        beside(
-            (2, grad_z, QKV, 3),
-        ),
-    )
-    act_y(BLK, 0)
+    act_y(BLK, 3)
     grad_z(QKV, 2)
-    grad_phase(DOWN)
-    act_y(BLK, 1)
-    grad_z(QKV, 1)
-    pre_phase(
-        beside(
-            (2, act_z, BLK, 0),
-            (3, grad_z, DOWN, 3),
-        ),
-    )
-    nrm_phase(
-        beside(
-            (2, act_z, BLK, 1),
-            (3, act_y, NRM, 0),
-        ),
-    )
-    act_y(NRM, 1)
-    grad_z(DOWN, 2)
-    grad_phase(OUT)
-    grad_z(DOWN, 1)
-    grad_phase(
-        UP,
-        beside(
-            (1, act_y, NRM, 2),
-            (1, act_z, NRM, 0),
-            (1, act_y, NRM, 3),
-            (3, grad_z, QKV, 0),
-        ),
-    )
-    act_z(NRM, 1)
-    grad_z(OUT, 3)
-    grad_z(UP, 3)
-    grad_z(UP, 2)
-    grad_last(QKV)
-    act_y(BLK, 3)
-    grad_z(OUT, 1)
-    act_y(BLK, 2)
-    grad_z(UP, 1)
+    grad_last(UP)
+    grad_z(DOWN, 0)
     act_gathered(TOK, tok_at)
     act_gathered(GRD, grd_at)
     for w in ws:
         w_sent(w)
     nrm_last()
+    grad_z(OUT, 1)
+    grad_z(QKV, 1)
+    grad_z(OUT, 2)
+    grad_z(QKV, 0)
     small_send()
-    grad_z(UP, 0)
+    input_last()
+    grad_z(OUT, 0)
+    grad_last(DOWN)
+    grad_last(QKV)
     blk_last()
-    grad_z(OUT, 0)
-    grad_z(DOWN, 0)
-    grad_z(OUT, 2)
-    grad_last(DOWN)
-    input_last()
-    grad_last(UP)
     for w in (QKV, OUT, DOWN):
         grad_sent(w)
     for name in (BLK, NRM):
         act_sent(name)
+    grad_last(OUT)
     small_last()
-    grad_last(OUT)
     grad_sent(UP)
     for k, where in enumerate(stat_where):
         send(m_["ST"], m_["STR"].at[k], sem_st + k, where).wait_send()

time: 100 us -> 99.2 us (level)
  no operation moved by 1% of the time
where the time goes in v5:
time: 99.2 us; the launch traced here: 99.1 us
  Pallas kernels  98.4 us (99%)
    pallas_call x1, Pallas kernels, on_device_fused(): pl.pallas_call(functools.partial(fused_kernel, s, names), out_shape=tuple...  96.4 us

profile of v5, /device:TPU:0, one launch (start us, length us, event | category | flops | bytes accessed | tf_op | source)
XLA Modules:
  0.0 99.1 jit_solution(561497372797858557)
XLA Ops:
  0.6 96.4 %shard_map.266 = (bf16[512,256]{1,0:T(8,128)(2,1)S(1)}, bf16[512,256]{1,0:T(8,128)(2,1)S(1)}, f32[3,128,256]{2,1,0:T(8,128)S(1)}, f32[128,1024]{1,0:T(8,128)S(1)...) custom-call(bf16[512,256]{1,0:T(8,128)(2,1)} %refs_0_.1, bf16[512,256]{1,0:T(8,128)(2,1)} %refs_1_.1, ...), custom_call_target="tpu_custom_call" | custom-call | tf_op jit(solution)/shard_map/pallas_call | solution.py:1413
  97.1 2.0 %shard_map.267 = (bf16[512,256]{1,0:T(8,128)(2,1)}, bf16[512,256]{1,0:T(8,128)(2,1)}, f32[3,128,256]{2,1,0:T(8,128)}, f32[128,1024]{1,0:T(8,128)}, f32[256,128]{...) custom-call(bf16[512,256]{1,0:T(8,128)(2,1)S(1)} %get-tuple-element., ...), custom_call_target="tpu_custom_call" | custom-call | tf_op jit(solution)/shard_map/pallas_call | solution.py:1446

commit v6 on v5

--- a/solution.py
+++ b/solution.py
@@ -1203,10 +1203,9 @@
         inv = IV[lanes(zl, s.rows), :]
         o_inp[...] = (own_g + inv * (scaled - mean1 - xhat * mean2)).astype(bf16)
 
+    w_own(OUT)
+    act_own(TOK, tok_at, "z")
     w_z(OUT, 3)
-    act_own(TOK, tok_at, "z")
-    w_own(QKV)
-    w_own(OUT)
     act_own(TOK, tok_at, "y")
     w_z(DOWN, 3)
     w_z(OUT, 1)
@@ -1214,12 +1213,13 @@
     w_z(QKV, 2)
     w_own(UP)
     w_relay(OUT)
+    w_z(QKV, 3)
+    w_own(QKV)
     act_arrive(TOK, tok_at, 1)
     w_z(DOWN, 1)
     act_arrive(TOK, tok_at, 0)
-    w_z(QKV, 3)
+    w_own(DOWN)
     act_own(GRD, grd_at, "y")
-    w_own(DOWN)
     w_forward(QKV, 2)
     w_z(QKV, 1)
     w_z(UP, 1)
@@ -1229,17 +1229,17 @@
     w_forward(OUT, 1)
     act_own(GRD, grd_at, "z")
     w_z(UP, 2)
+    act_arrive(TOK, tok_at, 2)
     w_relay(QKV)
     w_forward(QKV, 1)
-    act_arrive(TOK, tok_at, 2)
+    act_own(GRD, grd_at, "c")
     w_forward(UP, 1)
     w_forward(QKV, 3)
+    act_arrive(GRD, grd_at, 1)
     act_rest(TOK, tok_at)
     w_z(OUT, 2)
     table_phase()
     w_forward(UP, 2)
-    act_own(GRD, grd_at, "c")
-    act_arrive(GRD, grd_at, 1)
     w_relay(UP)
     w_z(DOWN, 2)
     act_arrive(GRD, grd_at, 0)
@@ -1261,16 +1261,13 @@
     up_phase(
         beside(
             (1, w_forward, DOWN, 3),
-            (3, act_rest, GRD, grd_at),
         ),
     )
+    act_rest(GRD, grd_at)
     grad_phase(DOWN)
     w_rest(DOWN)
-    pre_phase(
-        beside(
-            (1, w_rest, OUT),
-        ),
-    )
+    pre_phase()
+    w_rest(OUT)
     blk_phase(
         beside(
             (1, grad_z, DOWN, 3),
@@ -1281,12 +1278,12 @@
         UP,
         beside(
             (1, grad_z, DOWN, 2),
-            (2, act_y, BLK, 1),
         ),
     )
     act_y(BLK, 2)
     grad_z(DOWN, 1)
     act_z(BLK, 0)
+    act_y(BLK, 1)
     bwd_phase(
         beside(
             (2, grad_z, UP, 3),

time: 99.2 us -> 98.9 us (level)
  no operation moved by 1% of the time
where the time goes in v6:
time: 98.9 us; the launch traced here: 98.7 us
  Pallas kernels  98 us (99%)
    pallas_call x1, Pallas kernels, on_device_fused(): pl.pallas_call(functools.partial(fused_kernel, s, names), out_shape=tuple...  96.1 us

profile of v6, /device:TPU:0, one launch (start us, length us, event | category | flops | bytes accessed | tf_op | source)
XLA Modules:
  0.0 98.7 jit_solution(3456233645503283776)
XLA Ops:
  0.6 96.1 %shard_map.266 = (bf16[512,256]{1,0:T(8,128)(2,1)S(1)}, bf16[512,256]{1,0:T(8,128)(2,1)S(1)}, f32[3,128,256]{2,1,0:T(8,128)S(1)}, f32[128,1024]{1,0:T(8,128)S(1)...) custom-call(bf16[512,256]{1,0:T(8,128)(2,1)} %refs_0_.1, bf16[512,256]{1,0:T(8,128)(2,1)} %refs_1_.1, ...), custom_call_target="tpu_custom_call" | custom-call | tf_op jit(solution)/shard_map/pallas_call | solution.py:1410
  96.7 2.0 %shard_map.267 = (bf16[512,256]{1,0:T(8,128)(2,1)}, bf16[512,256]{1,0:T(8,128)(2,1)}, f32[3,128,256]{2,1,0:T(8,128)}, f32[128,1024]{1,0:T(8,128)}, f32[256,128]{...) custom-call(bf16[512,256]{1,0:T(8,128)(2,1)S(1)} %get-tuple-element., ...), custom_call_target="tpu_custom_call" | custom-call | tf_op jit(solution)/shard_map/pallas_call | solution.py:1443
